TPU v7x, 256 devices: a whole 4x4x8 slice. The times are simulated.
256 devices in a mesh: expert: 64 (over y, z, core), dp: 4 (over x).
Axes of the slice: x: 4, y: 4, z: 8, core: 2. Of those that a mesh axis runs over, the one named last changes fastest.
Arguments:
- tokens: bfloat16 [32768, 2048], P(('expert', 'dp')), may hold values from -6 to 6
- d_output: bfloat16 [32768, 2048], P(('expert', 'dp')), may hold values from -6 to 6
- expert_ids: int32 [32768, 8], P(('expert', 'dp')), may hold values from 0 to 63, all different within a row; in each aligned block of 128 rows (0 to 127, 128 to 255, ...) at most 24 rows name the same one
- gate_weights: bfloat16 [32768, 8], P(('expert', 'dp')), may hold values from 0.019897461 to 0.29882812
- pre_acts: bfloat16 [4, 64, 1536, 768], P('dp', 'expert'), may hold values from -6 to 6
- w_gate_up: bfloat16 [64, 2048, 768], P('expert'), may hold values from -0.125 to 0.125
- w_down: bfloat16 [64, 384, 2048], P('expert'), may hold values from -0.3125 to 0.3125
Outputs:
- token_grads: bfloat16 [32768, 2048], P(('expert', 'dp'))
- gate_grads: bfloat16 [32768, 8], P(('expert', 'dp'))
- gate_up_grads: float32 [64, 2048, 768], P('expert', 'dp')
- down_grads: float32 [64, 384, 2048], P('expert', None, 'dp')
Inputs may be any that keep to these rules, and one draw needn't show every extreme that they name: `expert_ids`: each token names 8 different experts; among the 128 tokens of one device (aligned blocks) no expert is named by more than 24 tokens, a bound that some block reaches.
All inputs are finite; a program needn't handle non-finite values.
Results may differ from a plain program's by a relative error of at most 0.0057.
Values may be sent and summed in bfloat16 or wider, within the bound.
A program may use at most 128 MiB of HBM per device.

v0:
```python
import jax
import jax.numpy as jnp
from jax import lax
from jax.sharding import PartitionSpec as P


def contract(left_side, right_side, left_dim, right_dim):
    return lax.dot_general(
        left_side,
        right_side,
        (((left_dim,), (right_dim,)), ((), ())),
        preferred_element_type=jnp.float32,
    )


def with_zero(values, picks):
    padding = jnp.zeros((1,) + values.shape[1:], values.dtype)
    return jnp.concatenate([values, padding], axis=0)[picks]


def expert_backward(grad_rows, gate_rows, saved_rows, gate_up_weight, down_weight):
    hidden = down_weight.shape[0]
    saved_vals = saved_rows.astype(jnp.float32)
    gate_input = saved_vals[:, :hidden]
    up_input = saved_vals[:, hidden:]
    logistic = jax.nn.sigmoid(gate_input)
    swish_val = gate_input * logistic
    activated = swish_val * up_input
    projected = contract(grad_rows, down_weight, 1, 1)
    gate_grad = jnp.sum(activated * projected, axis=1).astype(jnp.bfloat16)
    weights = gate_rows.astype(jnp.float32)[:, None]
    hidden_grad = weights * projected
    up_grad = hidden_grad * swish_val
    pre_grad = hidden_grad * up_input * logistic * (1.0 + gate_input * (1.0 - logistic))
    both_grad = jnp.concatenate([pre_grad, up_grad], axis=1).astype(jnp.bfloat16)
    scaled = (weights * activated).astype(jnp.bfloat16)
    down_grad = contract(scaled, grad_rows, 0, 0)
    route_grad = contract(both_grad, gate_up_weight, 1, 1).astype(jnp.bfloat16)
    return (gate_grad, both_grad, down_grad, route_grad)


def local_rows(received, local_index, sources, local_experts):
    shaped = received.reshape((sources, local_experts) + received.shape[1:])[:, local_index]
    return shaped.reshape((sources * received.shape[1],) + received.shape[2:])


def on_device(tokens, d_output, expert_ids, gate_weights, pre_acts, w_gate_up, w_down):
    sources = lax.axis_size("expert")
    tok_rows, model_width = tokens.shape
    top_count = expert_ids.shape[1]
    local_experts = w_down.shape[0]
    experts = local_experts * sources
    capacity = pre_acts.shape[2] // sources
    routes = tok_rows * top_count
    flat_ids = expert_ids.reshape(routes)
    onehot = (flat_ids[:, None] == jnp.arange(experts, dtype=jnp.int32)[None, :]).astype(jnp.int32)
    route_rank = jnp.sum((jnp.cumsum(onehot, axis=0) - onehot) * onehot, axis=1)
    position = flat_ids * capacity + route_rank
    slot_table = (
        jnp.full((experts * capacity,), routes, jnp.int32)
        .at[position]
        .set(jnp.arange(routes, dtype=jnp.int32))
    )
    token_pick = slot_table // top_count
    send_inputs = with_zero(tokens, token_pick).reshape(experts, capacity, model_width)
    send_grads = with_zero(d_output, token_pick).reshape(experts, capacity, model_width)
    send_gates = with_zero(gate_weights.reshape(routes), slot_table).reshape(experts, capacity)
    recv_inputs, recv_grads, recv_gates = (
        lax.all_to_all(send_inputs, "expert", split_axis=0, concat_axis=0, tiled=True),
        lax.all_to_all(send_grads, "expert", split_axis=0, concat_axis=0, tiled=True),
        lax.all_to_all(send_gates, "expert", split_axis=0, concat_axis=0, tiled=True),
    )
    local_index = 0
    grad_rows = local_rows(recv_grads, local_index, sources, local_experts)
    gate_rows = local_rows(recv_gates, local_index, sources, local_experts)
    saved_rows = pre_acts[0, local_index]
    gate_grad, both_grad, down_grad, route_grad = expert_backward(
        grad_rows, gate_rows, saved_rows, w_gate_up[local_index], w_down[local_index]
    )
    results = [(gate_grad, both_grad, down_grad, route_grad, None)]
    back_rows = jnp.stack(
        [record[3].reshape(sources, capacity, model_width) for record in results], axis=1
    ).reshape(experts, capacity, model_width)
    back_gates = jnp.stack(
        [record[0].reshape(sources, capacity) for record in results], axis=1
    ).reshape(experts, capacity)
    home_rows, home_gates = (
        lax.all_to_all(back_rows, "expert", split_axis=0, concat_axis=0, tiled=True),
        lax.all_to_all(back_gates, "expert", split_axis=0, concat_axis=0, tiled=True),
    )
    route_rows = home_rows.reshape(experts * capacity, model_width)[position].reshape(
        tok_rows, top_count, model_width
    )
    token_grads = jnp.sum(route_rows.astype(jnp.float32), axis=1).astype(jnp.bfloat16)
    gate_out = home_gates.reshape(experts * capacity)[position].reshape(tok_rows, top_count)
    local_index = 0
    input_rows = local_rows(recv_inputs, local_index, sources, local_experts)
    up_grads = [contract(input_rows, results[local_index][1], 0, 0)]
    gate_up_total = jnp.stack(up_grads, axis=0)
    down_total = jnp.stack([record[2] for record in results], axis=0)
    gate_up_share, down_share = (
        lax.psum_scatter(gate_up_total, "dp", scatter_dimension=1, tiled=True),
        lax.psum_scatter(down_total, "dp", scatter_dimension=2, tiled=True),
    )
    return (token_grads, gate_out, gate_up_share, down_share)


def solution(mesh):
    placed = (
        P(("expert", "dp"), None),
        P(("expert", "dp"), None),
        P(("expert", "dp"), None),
        P(("expert", "dp"), None),
        P("dp", "expert", None, None),
        P("expert", None, None),
        P("expert", None, None),
    )
    return jax.shard_map(
        on_device,
        mesh=mesh,
        in_specs=placed,
        out_specs=(
            P(("expert", "dp"), None),
            P(("expert", "dp"), None),
            P("expert", "dp", None),
            P("expert", None, "dp"),
        ),
        check_vma=False,
    )
```

profile of v0, /device:TPU:1, one launch (start us, length us, event | category | flops | bytes accessed | tf_op | source)
XLA Modules:
  0.0 576.9 jit_solution(7607548891776085508)
XLA Ops:
  10.9 31.1 %reduce-window.6 = s32[64,8,128]{2,1,0:T(8,128)S(1)} reduce-window(s32[64,8,128]{2,1,0:T(8,128)} %fusion.8, s32[]{:T(128)} %constant.13.clone.1), window={size=1x1x128 pad=0_0x0_0x127_0}, to_apply=%region_0.0 | reduce-window | flops 8323072 | bytes 524292 | tf_op jit(solution)/shard_map/reduce-window
  44.3 4.3 scatter_custom_fusion
  48.7 9.5 %gather_fusion = bf16[1536]{0:T(1024)(128)(2,1)S(1)} fusion(bf16[1025]{0:T(1024)(128)(2,1)S(1)} %pad_maximum_fusion.3, s32[2048]{0:T(1024)S(1)} %get-tuple-element.18), kind=kCustom, calls=%fused_computation | custom fusion | bytes 12288 | tf_op jit(solution)/shard_map/gather | solution.py:18
  58.9 13.1 %all-to-all-start = ((bf16[64,1,24]{2,1,0:T(2,128)(2,1)}), bf16[64,1,24]{2,1,0:T(2,128)(2,1)S(1)}, u32[]{:S(2)}, u32[]{:S(2)}) async-start(bf16[64,1,24]{2,1,0:T(2,128)(2,1)} %all_to_all.25), calls=%async_computation | async-start | bytes 65536 | tf_op jit(solution)/shard_map/all_to_all | solution.py:71
  72.0 1.9 concatenate.14
  73.9 13.9 %gather_fusion.1 = bf16[1536,2048]{1,0:T(8,128)(2,1)} fusion(bf16[129,2048]{1,0:T(8,128)(2,1)} %concatenate.14, s32[2048]{0:T(1024)S(1)} %get-tuple-element.17), kind=kCustom, calls=%fused_computation.1 | custom fusion | bytes 12589056 | tf_op jit(solution)/shard_map/gather | solution.py:18
  87.8 10.5 %all-to-all-start.1 = ((bf16[64,24,2048]{2,1,0:T(8,128)(2,1)}), bf16[64,24,2048]{2,1,0:T(8,128)(2,1)}, u32[]{:S(2)}, u32[]{:S(2)}) async-start(bf16[64,24,2048]{2,1,0:T(8,128)(2,1)} %bitcast.48), calls=%async_computation.1 | async-start | bytes 12582912 | tf_op jit(solution)/shard_map/all_to_all | solution.py:70
  98.3 1.9 concatenate.16
  100.2 13.8 %gather_fusion.4 = bf16[1536,2048]{1,0:T(8,128)(2,1)} fusion(bf16[129,2048]{1,0:T(8,128)(2,1)} %concatenate.16, s32[2048]{0:T(1024)S(1)} %get-tuple-element.17), kind=kCustom, calls=%fused_computation.4 | custom fusion | bytes 12589056 | tf_op jit(solution)/shard_map/gather | solution.py:18
  114.0 125.1 %all-to-all-done.1 = bf16[64,24,2048]{2,1,0:T(8,128)(2,1)} async-done(((bf16[64,24,2048]{2,1,0:T(8,128)(2,1)}), bf16[64,24,2048]{2,1,0:T(8,128)(2,1)}, u32[]{:S(2)}, u32[]{:S(2)}) %all-to-all-start.1) | async-done | bytes 6291488 | tf_op jit(solution)/shard_map/all_to_all | solution.py:70
  239.1 6.0 %all-to-all-start.4 = ((bf16[64,24,2048]{2,1,0:T(8,128)(2,1)}), bf16[64,24,2048]{2,1,0:T(8,128)(2,1)}, u32[]{:S(2)}, u32[]{:S(2)}) async-start(bf16[64,24,2048]{2,1,0:T(8,128)(2,1)} %bitcast.47), calls=%async_computation.4 | async-start | bytes 12582912 | tf_op jit(solution)/shard_map/all_to_all | solution.py:69
  245.3 4.3 copy.27
  249.6 4.5 bitcast_convert_fusion
  254.3 8.6 %convolution_bitcast_fusion.1 = f32[1,384,2048]{2,1,0:T(8,128)} fusion(bf16[1536,2048]{1,0:T(8,128)(2,1)} %bitcast.5, f32[1536]{0:T(1024)S(1)} %reshape.112, f32[1536,768]{0,1:T(8,128)} %bitcast_convert_fusion), kind=kOutput, calls=%fused_computation.10 | convolution fusion | flops 2420047872 | bytes 14161920 | tf_op jit(solution)/shard_map/dot_general | solution.py:8
  263.0 9.5 %multiply_convert_fusion.2 = (bf16[1536,384]{0,1:T(8,128)(2,1)}, bf16[1536,384]{0,1:T(8,128)(2,1)}, bf16[1536]{0:T(1024)(128)(2,1)S(1)}) fusion(f32[1536,768]{0,1:T(8,128)} %bitcast_convert_fusion, f32[1536]{0:T(1024)S(1)} %reshape.112, bf16[1536,2048]{1,0:T(8,128)(2,1)} %bitcast.5, bf16[1,384,2048]{2,1,0:T(8,128)(2,1)} %param.13), kind=kOutput, calls=%fused_computation.16 | convolution fusion | flops 2425944576 | bytes 14951424 | tf_op jit(solution)/shard_map/dot_general | solution.py:8
  273.2 112.7 %all-to-all-done.4 = bf16[64,24,2048]{2,1,0:T(8,128)(2,1)} async-done(((bf16[64,24,2048]{2,1,0:T(8,128)(2,1)}), bf16[64,24,2048]{2,1,0:T(8,128)(2,1)}, u32[]{:S(2)}, u32[]{:S(2)}) %all-to-all-start.4) | async-done | bytes 6291488 | tf_op jit(solution)/shard_map/all_to_all | solution.py:69
  385.9 5.8 %all-to-all-start.3 = ((bf16[64,1,24]{2,1,0:T(2,128)(2,1)}), bf16[64,1,24]{2,1,0:T(2,128)(2,1)S(1)}, u32[]{:S(2)}, u32[]{:S(2)}) async-start(bf16[64,1,24]{2,1,0:T(2,128)(2,1)} %convert_element_type.58), calls=%async_computation.3 | async-start | bytes 65536 | tf_op jit(solution)/shard_map/all_to_all | solution.py:89
  391.7 8.8 %convolution_convert_fusion = bf16[1536,2048]{1,0:T(8,128)(2,1)} fusion(bf16[1,2048,768]{2,1,0:T(8,128)(2,1)S(1)} %copy-done, bf16[1536,384]{0,1:T(8,128)(2,1)} %get-tuple-element.13, bf16[1536,384]{0,1:T(8,128)(2,1)} %get-tuple-element.12), kind=kOutput, calls=%fused_computation.6 | convolution fusion | flops 4839702528 | bytes 11796480 | tf_op jit(solution)/shard_map/dot_general | solution.py:8
  400.9 10.0 %all-to-all-start.2 = ((bf16[64,24,2048]{2,1,0:T(8,128)(2,1)}), bf16[64,24,2048]{2,1,0:T(8,128)(2,1)}, u32[]{:S(2)}, u32[]{:S(2)}) async-start(bf16[64,24,2048]{2,1,0:T(8,128)(2,1)} %bitcast.49), calls=%async_computation.2 | async-start | bytes 12582912 | tf_op jit(solution)/shard_map/all_to_all | solution.py:88
  411.2 9.5 %convolution_bitcast_fusion = f32[1,2048,768]{2,1,0:T(8,128)} fusion(bf16[1536,2048]{1,0:T(8,128)(2,1)} %bitcast.14, bf16[1536,384]{0,1:T(8,128)(2,1)} %get-tuple-element.13, bf16[1536,384]{0,1:T(8,128)(2,1)} %get-tuple-element.12), kind=kOutput, calls=%fused_computation.8 | convolution fusion | flops 4836556800 | bytes 14942208 | tf_op jit(solution)/shard_map/dot_general | solution.py:8
  421.0 6.8 %gather_fusion.3 = bf16[1024]{0:T(1024)(128)(2,1)S(1)} fusion(bf16[1536]{0:T(1024)(128)(2,1)S(1)} %reshape.109, s32[1024]{0:T(1024)S(1)} %broadcast_clamp_fusion), kind=kCustom, calls=%fused_computation.3 | custom fusion | bytes 8192 | tf_op jit(solution)/shard_map/gather | solution.py:95
  428.6 123.2 %all-to-all-done.2 = bf16[64,24,2048]{2,1,0:T(8,128)(2,1)} async-done(((bf16[64,24,2048]{2,1,0:T(8,128)(2,1)}), bf16[64,24,2048]{2,1,0:T(8,128)(2,1)}, u32[]{:S(2)}, u32[]{:S(2)}) %all-to-all-start.2) | async-done | bytes 6291488 | tf_op jit(solution)/shard_map/all_to_all | solution.py:88
  551.8 12.4 %gather_fusion.2 = bf16[1024,2048]{1,0:T(8,128)(2,1)} fusion(bf16[1536,2048]{1,0:T(8,128)(2,1)} %bitcast.11, s32[1024]{0:T(1024)S(1)} %broadcast_clamp_fusion), kind=kCustom, calls=%fused_computation.2 | custom fusion | bytes 8392704 | tf_op jit(solution)/shard_map/gather | solution.py:91
  564.2 5.9 %bitcast_reduce_fusion = bf16[128,2048]{1,0:T(8,128)(2,1)} fusion(bf16[1024,2048]{1,0:T(8,128)(2,1)} %gather_fusion.2), kind=kLoop, calls=%fused_computation.7 | loop fusion | flops 1835008 | bytes 4718592 | tf_op jit(solution)/shard_map/reduce_sum | solution.py:94
  (40 shorter events, 9.6 us)
Async XLA Ops:
  7.2 384.5 %copy-start = (bf16[1,2048,768]{2,1,0:T(8,128)(2,1)S(1)}, bf16[1,2048,768]{2,1,0:T(8,128)(2,1)}, u32[]{:S(2)}) copy-start(bf16[1,2048,768]{2,1,0:T(8,128)(2,1)} %param.12) | copy-start | bytes 9437188
  58.9 28.9 %all-to-all-start = ((bf16[64,1,24]{2,1,0:T(2,128)(2,1)}), bf16[64,1,24]{2,1,0:T(2,128)(2,1)S(1)}, u32[]{:S(2)}, u32[]{:S(2)}) async-start(bf16[64,1,24]{2,1,0:T(2,128)(2,1)} %all_to_all.25), calls=%async_computation | async-start | bytes 65536 | tf_op jit(solution)/shard_map/all_to_all | solution.py:71
  87.8 151.3 %all-to-all-start.1 = ((bf16[64,24,2048]{2,1,0:T(8,128)(2,1)}), bf16[64,24,2048]{2,1,0:T(8,128)(2,1)}, u32[]{:S(2)}, u32[]{:S(2)}) async-start(bf16[64,24,2048]{2,1,0:T(8,128)(2,1)} %bitcast.48), calls=%async_computation.1 | async-start | bytes 12582912 | tf_op jit(solution)/shard_map/all_to_all | solution.py:70
  239.1 146.8 %all-to-all-start.4 = ((bf16[64,24,2048]{2,1,0:T(8,128)(2,1)}), bf16[64,24,2048]{2,1,0:T(8,128)(2,1)}, u32[]{:S(2)}, u32[]{:S(2)}) async-start(bf16[64,24,2048]{2,1,0:T(8,128)(2,1)} %bitcast.47), calls=%async_computation.4 | async-start | bytes 12582912 | tf_op jit(solution)/shard_map/all_to_all | solution.py:69
  245.1 325.0 %reduce-scatter.5.cloned.1.call-start = ((), (), s32[]{:S(2)}) async-start(), calls=%async_computation.8 | async-start | bytes 3932160 | tf_op jit(solution)/shard_map/reduce_scatter | solution.py:103
  385.9 15.0 %all-to-all-start.3 = ((bf16[64,1,24]{2,1,0:T(2,128)(2,1)}), bf16[64,1,24]{2,1,0:T(2,128)(2,1)S(1)}, u32[]{:S(2)}, u32[]{:S(2)}) async-start(bf16[64,1,24]{2,1,0:T(2,128)(2,1)} %convert_element_type.58), calls=%async_computation.3 | async-start | bytes 65536 | tf_op jit(solution)/shard_map/all_to_all | solution.py:89
  400.9 150.9 %all-to-all-start.2 = ((bf16[64,24,2048]{2,1,0:T(8,128)(2,1)}), bf16[64,24,2048]{2,1,0:T(8,128)(2,1)}, u32[]{:S(2)}, u32[]{:S(2)}) async-start(bf16[64,24,2048]{2,1,0:T(8,128)(2,1)} %bitcast.49), calls=%async_computation.2 | async-start | bytes 12582912 | tf_op jit(solution)/shard_map/all_to_all | solution.py:88
  411.0 159.1 %reduce-scatter.3.cloned.1.call-start = ((), (), s32[]{:S(2)}) async-start(), calls=%async_computation.7 | async-start | bytes 7864320 | tf_op jit(solution)/shard_map/reduce_scatter | solution.py:102
Sparse Core Ops, SparseCore 0:
  263.1 41.7 reduce-scatter.4
  420.9 67.3 reduce-scatter.2
where the time goes:
time: 579 us; the launch traced here: 577 us
  waiting for transfers between devices  361 us (62%)
  local copies, waits for them, and re-layouts  75.4 us (13%)
  starting transfers between devices  45.9 us (8%)
  other arithmetic  43.5 us (8%)
  matrix products  36.5 us (6%)
  between operations  14.2 us (2%)
    all_to_all x1, waiting for transfers between devices, on_device(): lax.all_to_all(send_grads, 'expert', split_axis=0, concat_axis=0, tiled=T...  125 us
    all_to_all x1, waiting for transfers between devices, on_device(): lax.all_to_all(back_rows, 'expert', split_axis=0, concat_axis=0, tiled=True)  123 us
    all_to_all x1, waiting for transfers between devices, on_device(): lax.all_to_all(send_inputs, 'expert', split_axis=0, concat_axis=0, tiled=...  113 us
    gather x3, local copies, waits for them, and re-layouts, with_zero(): return jnp.concatenate([values, padding], axis=0)[picks]  37.1 us
    dot_general x4, matrix products, contract(): lax.dot_general(left_side, right_side, (((left_dim,), (right_dim,)), ((),...  36.5 us
    another operation x3, other arithmetic  31.3 us
    all_to_all x1, starting transfers between devices, on_device(): lax.all_to_all(send_gates, 'expert', split_axis=0, concat_axis=0, tiled=T...  13.1 us
    gather x1, local copies, waits for them, and re-layouts, on_device(): home_rows.reshape(experts * capacity, model_width)[position]  12.4 us
  transfers between devices with their start and end apart: 7, of which 4 were waited for; matrix products, arithmetic and copies ran while one was open for 18% of the time, Pallas kernels for 0%

commit v1 on v0

v1 whole, which is shorter than its diff:
```python
import jax
import jax.numpy as jnp
from jax import lax
from jax.experimental import pallas as pl
from jax.experimental.pallas import tpu as pltpu
from jax.sharding import Mesh, PartitionSpec as P

MESH = pl.DeviceIdType.MESH
NY, NZ, NC, NX = 4, 8, 2, 4
TOK, TOPK, D, FF, CAP = 128, 8, 2048, 384, 24
HALF = D // 2
TILE = min(256, HALF)
PAIR = 2 * TOK
SEG = 2 * CAP
PEERS = NY * NC
ROWS = PEERS * SEG
YROWS = NZ * SEG
SLOTS = NY * YROWS


def contract(left_side, right_side, left_dim, right_dim):
    return lax.dot_general(
        left_side,
        right_side,
        (((left_dim,), (right_dim,)), ((), ())),
        preferred_element_type=jnp.float32,
    )


def plane_barrier(y, z, c):
    barrier = pltpu.get_barrier_semaphore()
    for dy in range(NY):
        for dc in range(NC):
            if dy or dc:
                pl.semaphore_signal(
                    barrier,
                    inc=1,
                    device_id={"y": (y + dy) % NY, "c": (c + dc) % NC},
                    device_id_type=MESH,
                )
    for dz in (1, NZ - 1):
        pl.semaphore_signal(barrier, inc=1, device_id={"z": (z + dz) % NZ}, device_id_type=MESH)
    pl.semaphore_wait(barrier, PEERS - 1 + 2)


def remote(src, dst, send_sem, recv_sem, where):
    return pltpu.make_async_remote_copy(
        src_ref=src, dst_ref=dst, send_sem=send_sem, recv_sem=recv_sem, device_id=where, device_id_type=MESH
    )


def place():
    return lax.axis_index("y"), lax.axis_index("z"), lax.axis_index("c")


def table(ids, gates, c):
    lane = lax.broadcasted_iota(jnp.int32, (TOK, 128), 1)
    expert = ((lane // 2) % NY) * (NZ * NC) + (lane // 16) * NC + lane % 2
    second = (lane // 8) % 2
    named = jnp.zeros((TOK, 128), jnp.float32)
    weight = jnp.zeros((TOK, 128), jnp.float32)
    for k in range(TOPK):
        hit = ids[:, k : k + 1] == expert
        named += jnp.where(hit, 1.0, 0.0)
        weight += jnp.where(hit, gates[:, k : k + 1], 0.0)
    named = named.astype(jnp.bfloat16)
    weight = weight.astype(jnp.bfloat16)
    row = lax.broadcasted_iota(jnp.int32, (TOK, TOK), 0)
    col = lax.broadcasted_iota(jnp.int32, (TOK, TOK), 1)
    before = jnp.where(row < col, 1.0, 0.0).astype(jnp.bfloat16)
    same = jnp.where(row == col, 1.0, 0.0).astype(jnp.bfloat16)
    rank_t = contract(named, before, 0, 0)
    named_t = contract(named, same, 0, 0)
    weight_t = contract(weight, same, 0, 0)
    rank_t = jnp.where(named_t > 0.5, rank_t + (c * CAP).astype(jnp.float32), -1.0)
    second_t = (lax.broadcasted_iota(jnp.int32, (128, TOK), 0) // 8) % 2
    return jnp.where(second_t == 1, weight_t, rank_t).astype(jnp.bfloat16)


def dispatch_kernel(
    ids_ref, gates_ref, d_ref, t_ref, gd_out, tok_out, pick_ref,
    meta, blocks, staged, scaled, load_sem, pair_send, pair_recv, ring_send, ring_recv, out_send, out_recv,
):
    y, z, c = place()
    partner = {"c": 1 - c}
    up, down = {"z": (z + 1) % NZ}, {"z": (z + NZ - 1) % NZ}
    mine = pl.ds(pl.multiple_of(c * TOK, TOK), TOK)
    my_half = pl.ds(pl.multiple_of(c * HALF, HALF), HALF)
    its_half = pl.ds(pl.multiple_of((1 - c) * HALF, HALF), HALF)
    sources = (d_ref, t_ref)
    outs = (gd_out, tok_out)

    loads = [
        pltpu.make_async_copy(sources[a].at[:, my_half], blocks.at[a, z, mine, :], load_sem.at[a]) for a in range(2)
    ]
    for load in loads:
        load.start()
    meta[z, c] = table(ids_ref[...], gates_ref[...].astype(jnp.float32), c)
    plane_barrier(y, z, c)
    pairs = [
        remote(meta.at[z, c], meta.at[z, c], pair_send.at[2], pair_recv.at[2], partner),
        remote(sources[0].at[:, its_half], blocks.at[0, z, mine, :], pair_send.at[0], pair_recv.at[0], partner),
        remote(sources[1].at[:, its_half], blocks.at[1, z, mine, :], pair_send.at[1], pair_recv.at[1], partner),
    ]
    for copy in pairs:
        copy.start()

    def ring(a, step, direction):
        where = up if direction == 0 else down
        block = (z + NZ - step) % NZ if direction == 0 else (z + step) % NZ
        if a == 2:
            ref = meta.at[block, direction] if step == 3 else meta.at[block]
        else:
            ref = blocks.at[a, block, pl.ds(direction * TOK, TOK), :] if step == 3 else blocks.at[a, block]
        return remote(ref, ref, ring_send.at[a, step, direction], ring_recv.at[a, step, direction], where)

    def pick_block(block):
        rows = jnp.concatenate(
            [meta[block, i, pl.ds(pl.multiple_of(z * 16, 16), 16), :].astype(jnp.float32) for i in range(2)], axis=1
        )
        rank, weight = rows[:8, :], rows[8:, :]
        slot = lax.broadcasted_iota(jnp.int32, (PEERS, SEG, PAIR), 1).astype(jnp.float32)
        hit = jnp.where(rank[:, None, :] == slot, 1.0, 0.0)
        pick_ref[block] = hit.reshape(ROWS, PAIR).astype(jnp.bfloat16)
        scaled[...] = (hit * weight[:, None, :]).reshape(ROWS, PAIR).astype(jnp.bfloat16)

    def send_block(a, block):
        if a == 0:
            pick_block(block)

        def tile(i, carry):
            cols = pl.ds(pl.multiple_of(i * TILE, TILE), TILE)
            matrix = scaled[...] if a == 0 else pick_ref[block]
            staged[a, block, :, cols] = contract(matrix, blocks[a, block, :, cols], 1, 0).astype(jnp.bfloat16)
            return carry

        lax.fori_loop(0, HALF // TILE, tile, 0)
        at = outs[a].at[pl.ds(pl.multiple_of(y * YROWS + block * SEG, SEG), SEG), my_half]
        for dy in (1, 3, 2, 0):
            for dc in range(NC):
                py, pc = (y + dy) % NY, (c + dc) % NC
                src = staged.at[a, block, pl.ds(pl.multiple_of((py * NC + pc) * SEG, SEG), SEG), :]
                if dy or dc:
                    remote(src, at, out_send.at[a], out_recv.at[a], {"y": py, "c": pc}).start()
                else:
                    pltpu.make_async_copy(src, at, out_recv.at[a]).start()

    def begin(a):
        loads[a].wait()
        pairs[a + 1].wait_recv()
        for direction in range(2):
            ring(a, 0, direction).start()

    pairs[0].wait_recv()
    for direction in range(2):
        ring(2, 0, direction).start()
    begin(0)
    for a in range(2):
        send_block(a, z)
        for step in range(4):
            for direction in range(2):
                if a == 0:
                    ring(2, step, direction).wait_recv()
                ring(a, step, direction).wait_recv()
            if step < 3:
                for direction in range(2):
                    if a == 0:
                        ring(2, step + 1, direction).start()
                    ring(a, step + 1, direction).start()
            elif a == 0:
                begin(1)
            send_block(a, (z + NZ - 1 - step) % NZ)
            if step < 3:
                send_block(a, (z + 1 + step) % NZ)
    for copy in pairs:
        copy.wait_send()
    for a in range(3):
        for step in range(4):
            for direction in range(2):
                ring(a, step, direction).wait_send()
    for a in range(2):
        most = staged.at[a, pl.ds(0, PEERS - 1)]
        pltpu.make_async_copy(most, most, out_send.at[a]).wait()
        pltpu.make_async_copy(outs[a], outs[a], out_recv.at[a]).wait()


def combine_kernel(
    rows_ref, pick_ref, out_ref,
    arrived, going, coming, last, out_send, out_recv, ring_send, ring_recv, pair_send, pair_recv,
):
    y, z, c = place()
    partner = {"c": 1 - c}
    up, down = {"z": (z + 1) % NZ}, {"z": (z + NZ - 1) % NZ}
    my_half = pl.ds(pl.multiple_of(c * HALF, HALF), HALF)
    its_half = pl.ds(pl.multiple_of((1 - c) * HALF, HALF), HALF)
    plane_barrier(y, z, c)
    at = pl.ds(pl.multiple_of((y * NC + c) * SEG, SEG), SEG)
    order = (4, 5, 3, 6, 2, 7, 1, 0)
    for n, dz in enumerate(order):
        block = (z + dz) % NZ
        for dy in (1, 3, 2, 0):
            for dc in range(NC):
                py, pc = (y + dy) % NY, (c + dc) % NC
                src = rows_ref.at[
                    pl.ds(pl.multiple_of(py * YROWS + block * SEG, SEG), SEG), pl.ds(pl.multiple_of(pc * HALF, HALF), HALF)
                ]
                if dy or dc:
                    remote(src, arrived.at[block, at, :], out_send, out_recv.at[n], {"y": py, "c": pc}).start()
                else:
                    pltpu.make_async_copy(src, arrived.at[block, at, :], out_recv.at[n]).start()

    def ring(step, direction):
        rows = pl.ds(direction * TOK, TOK) if step == 0 else pl.ds(0, PAIR)
        return remote(
            going.at[direction, step, rows, :],
            coming.at[direction, step, rows, :],
            ring_send.at[direction, step],
            ring_recv.at[direction, step],
            up if direction == 0 else down,
        )

    def ready(n):
        block = arrived.at[(z + order[n]) % NZ]
        pltpu.make_async_copy(block, block, out_recv.at[n]).wait()

    def partial(n, add, store):
        block = (z + order[n]) % NZ

        def tile(i, carry):
            cols = pl.ds(pl.multiple_of(i * TILE, TILE), TILE)
            store(cols, add(cols, contract(pick_ref[block], arrived[block, :, cols], 0, 0)))
            return carry

        lax.fori_loop(0, HALF // TILE, tile, 0)

    def store_first(cols, value):
        value = value.astype(jnp.bfloat16)
        going[0, 0, :TOK, cols] = value[:TOK]
        going[1, 0, TOK:, cols] = value[TOK:]

    ready(0)
    partial(0, lambda cols, value: value, store_first)
    ring(0, 0).start()
    ring(0, 1).start()
    for step in range(1, 4):
        for direction in (1, 0):
            n = 2 * step - 1 if direction == 1 else 2 * step
            ready(n)
            ring(step - 1, direction).wait_recv()

            def add(cols, value):
                if step > 1:
                    return value + coming[direction, step - 1, :, cols].astype(jnp.float32)
                part = coming[direction, 0, pl.ds(direction * TOK, TOK), cols].astype(jnp.float32)
                if direction == 0:
                    return jnp.concatenate([value[:TOK] + part, value[TOK:]], axis=0)
                return jnp.concatenate([value[:TOK], value[TOK:] + part], axis=0)

            def store(cols, value):
                going[direction, step, :, cols] = value.astype(jnp.bfloat16)

            partial(n, add, store)
            ring(step, direction).start()
    ready(7)
    for direction in range(2):
        ring(3, direction).wait_recv()

    def add_both(cols, value):
        return value + coming[0, 3, :, cols].astype(jnp.float32) + coming[1, 3, :, cols].astype(jnp.float32)

    def store_last(cols, value):
        going[0, 0, :, cols] = value.astype(jnp.bfloat16)

    for direction in range(2):
        ring(0, direction).wait_send()
    partial(7, add_both, store_last)
    mine = pl.ds(pl.multiple_of(c * TOK, TOK), TOK)
    its = pl.ds(pl.multiple_of((1 - c) * TOK, TOK), TOK)
    swap = remote(going.at[0, 0, its, :], last, pair_send, pair_recv, partner)
    swap.start()
    out_ref[:, my_half] = going[0, 0, mine, :]
    swap.wait_recv()
    out_ref[:, its_half] = last[...]
    swap.wait_send()
    for step in range(1, 4):
        for direction in range(2):
            ring(step, direction).wait_send()
    most = arrived.at[pl.ds(0, PEERS - 1)]
    pltpu.make_async_copy(most, most, out_send).wait()


ANY = pl.BlockSpec(memory_space=pl.ANY)
VMEM = pl.BlockSpec(memory_space=pltpu.VMEM)
DMA = pltpu.SemaphoreType.DMA


def dispatch(expert_ids, gate_weights, d_output, tokens):
    rows = jax.ShapeDtypeStruct((SLOTS, D), jnp.bfloat16)
    return pl.pallas_call(
        dispatch_kernel,
        out_shape=(rows, rows, jax.ShapeDtypeStruct((NZ, ROWS, PAIR), jnp.bfloat16)),
        in_specs=[VMEM, VMEM, ANY, ANY],
        out_specs=(ANY, ANY, VMEM),
        scratch_shapes=[
            pltpu.VMEM((NZ, NC, 128, TOK), jnp.bfloat16),
            pltpu.VMEM((2, NZ, PAIR, HALF), jnp.bfloat16),
            pltpu.VMEM((2, NZ, ROWS, HALF), jnp.bfloat16),
            pltpu.VMEM((ROWS, PAIR), jnp.bfloat16),
            DMA((2,)),
            DMA((3,)),
            DMA((3,)),
            DMA((3, 4, 2)),
            DMA((3, 4, 2)),
            DMA((2,)),
            DMA((2,)),
        ],
        compiler_params=pltpu.CompilerParams(collective_id=0, has_side_effects=True),
        name="dispatch",
    )(expert_ids, gate_weights, d_output, tokens)


def combine(route_rows, pick):
    return pl.pallas_call(
        combine_kernel,
        out_shape=jax.ShapeDtypeStruct((TOK, D), jnp.bfloat16),
        in_specs=[ANY, VMEM],
        out_specs=VMEM,
        scratch_shapes=[
            pltpu.VMEM((NZ, ROWS, HALF), jnp.bfloat16),
            pltpu.VMEM((2, 4, PAIR, HALF), jnp.bfloat16),
            pltpu.VMEM((2, 4, PAIR, HALF), jnp.bfloat16),
            pltpu.VMEM((TOK, HALF), jnp.bfloat16),
            DMA,
            DMA((8,)),
            DMA((2, 4)),
            DMA((2, 4)),
            DMA,
            DMA,
        ],
        compiler_params=pltpu.CompilerParams(collective_id=1, has_side_effects=True),
        name="combine",
    )(route_rows, pick)


def on_device(tokens, d_output, expert_ids, gate_weights, pre_acts, w_gate_up, w_down):
    grad_rows, input_rows, pick = dispatch(expert_ids, gate_weights, d_output, tokens)
    saved = pre_acts[0, 0]
    gate_input = saved[:, :FF].astype(jnp.float32)
    up_input = saved[:, FF:].astype(jnp.float32)
    logistic = jax.nn.sigmoid(gate_input)
    swish = gate_input * logistic
    activated = swish * up_input
    hidden_grad = contract(grad_rows, w_down[0], 1, 1)
    gate_dot = jnp.sum(activated * hidden_grad, axis=1).astype(jnp.bfloat16)
    up_grad = hidden_grad * swish
    pre_grad = hidden_grad * up_input * logistic * (1.0 + gate_input * (1.0 - logistic))
    both_grad = jnp.concatenate([pre_grad, up_grad], axis=1).astype(jnp.bfloat16)
    route_grad = contract(both_grad, w_gate_up[0], 1, 1).astype(jnp.bfloat16)
    down_grad = contract(activated.astype(jnp.bfloat16), grad_rows, 0, 0)
    gate_up_grad = contract(input_rows, both_grad, 0, 0)
    down_share = lax.psum_scatter(down_grad[None], "dp", scatter_dimension=2, tiled=True)
    gate_up_share = lax.psum_scatter(gate_up_grad[None], "dp", scatter_dimension=1, tiled=True)
    token_grads = combine(route_grad, pick)

    home = lax.all_to_all(
        gate_dot.reshape(NY * NZ * NC, 1, CAP), ("y", "z", "c"), split_axis=0, concat_axis=0, tiled=True
    ).reshape(NY * NZ * NC, CAP)
    experts = jnp.arange(NY * NZ * NC, dtype=jnp.int32)
    hit = (expert_ids[:, :, None] == experts).astype(jnp.bfloat16)
    named = jnp.sum(hit, axis=1)
    order = jnp.arange(TOK, dtype=jnp.int32)
    before = (order[:, None] > order[None, :]).astype(jnp.bfloat16)
    rank = contract(before, named, 1, 0)
    slots = jnp.arange(CAP, dtype=jnp.float32)
    dense = jnp.sum(
        jnp.where(rank[:, :, None] == slots, home.astype(jnp.float32)[None], 0.0), axis=2
    )
    picked = jnp.sum(jnp.where(expert_ids[:, :, None] == experts, dense[:, None, :], 0.0), axis=2)
    gate_grads = (picked / gate_weights.astype(jnp.float32)).astype(jnp.bfloat16)
    return token_grads, gate_grads, gate_up_share, down_share


def solution(mesh):
    grid = Mesh(mesh.devices.reshape(NY, NZ, NC, NX), ("y", "z", "c", "dp"))
    expert = ("y", "z", "c")
    token = P(expert + ("dp",), None)
    return jax.shard_map(
        on_device,
        mesh=grid,
        in_specs=(
            token, token, token, token,
            P("dp", expert, None, None), P(expert, None, None), P(expert, None, None),
        ),
        out_specs=(token, token, P(expert, "dp", None), P(expert, None, "dp")),
        check_vma=False,
    )
```

time: 579 us -> 311 us (0.54)
  waiting for transfers between devices: 361 us -> 0.04 us
  Pallas kernels: 0 us -> 243 us
  local copies, waits for them, and re-layouts: 75.4 us -> 11.3 us
  other arithmetic: 43.5 us -> 0.99 us
  starting transfers between devices: 45.9 us -> 6.39 us
    all_to_all x5 -> x1, waiting for transfers between devices: 361 us -> 0.01 us  [on_device(): lax.all_to_all(gate_dot.reshape(NY * NZ * NC, 1, CAP), ('y', 'z', 'c'), s...]
    pallas_call x0 -> x2, Pallas kernels: none -> 243 us  [the longest x1 158 us: dispatch(): pl.pallas_call(dispatch_kernel, out_shape=(rows, rows, jax.ShapeDtypeStru...]
    gather x5 -> x0, local copies, waits for them, and re-layouts: 56.4 us -> none  [the longest x3 37.1 us: with_zero(): return jnp.concatenate([values, padding], axis=0)[picks]]
    all_to_all x5 -> x1, starting transfers between devices: 45.4 us -> 6.13 us  [on_device(): lax.all_to_all(gate_dot.reshape(NY * NZ * NC, 1, CAP), ('y', 'z', 'c'), s...]
    another operation x3 -> x0, other arithmetic: 31.3 us -> none
    dot_general x4 -> x5, matrix products: 36.5 us -> 35 us  [contract(): lax.dot_general(left_side, right_side, (((left_dim,), (right_dim,)), ((),...]
  transfers between devices with their start and end apart: 7 -> 3, of which waited for: 4 -> 0; matrix products, arithmetic and copies ran while one was open for 18% -> 9% of each run, Pallas kernels for 0% -> 27%
where the time goes in v1:
time: 311 us
  Pallas kernels  243 us (78%)
  matrix products  35 us (11%)
  between operations  14.2 us (5%)
  local copies, waits for them, and re-layouts  11.3 us (4%)
  starting transfers between devices  6.39 us (2%)
    pallas_call x1, Pallas kernels, dispatch(): pl.pallas_call(dispatch_kernel, out_shape=(rows, rows, jax.ShapeDtypeStru...  158 us
    pallas_call x1, Pallas kernels, combine(): pl.pallas_call(combine_kernel, out_shape=jax.ShapeDtypeStruct((TOK, D), j...  85.4 us
    dot_general x5, matrix products, contract(): lax.dot_general(left_side, right_side, (((left_dim,), (right_dim,)), ((),...  35 us
    unnamed x14, local copies, waits for them, and re-layouts  10.5 us
  transfers between devices with their start and end apart: 3, of which 0 were waited for; matrix products, arithmetic and copies ran while one was open for 9% of the time, Pallas kernels for 27%

profile of v1, /device:TPU:1, one launch (start us, length us, event | category | flops | bytes accessed | tf_op | source)
XLA Modules:
  0.0 310.9 jit_solution(10945004830651389806)
XLA Ops:
  7.2 0.0 copy-start
  7.2 0.0 reduce-scatter.5.cloned.1.call-start
  7.2 1.6 copy.28.gates_ref
  8.8 1.4 copy.27.ids_ref
  10.2 4.3 %copy.29 = bf16[1,1,1536,768]{2,3,1,0:T(8,128)(2,1)} copy(bf16[1,1,1536,768]{3,2,1,0:T(8,128)(2,1)} %param.11) | data formatting | bytes 4718592 | tf_op args[4]
  14.5 157.6 %dispatch.1 = (bf16[1536,2048]{1,0:T(8,128)(2,1)}, bf16[1536,2048]{1,0:T(8,128)(2,1)}, bf16[8,384,256]{2,1,0:T(8,128)(2,1)}) custom-call(s32[128,8]{1,0:T(8,128)} %copy.27.ids_ref, bf16[128,8]{1,0:T(8,128)(2,1)} %copy.28.gates_ref, bf16[128,2048]{1,0:T(8,128)(2,1)} %d_ref.1, bf16[128,2048]{1,0:T(8,128)(2,1)} %t_ref.1), custom_call_target="tpu_custom_call" | custom-call | tf_op jit(solution)/shard_map/dispatch/pallas_call | solution.py:299
  172.1 8.0 %convolution_bitcast_fusion.1 = f32[1,384,2048]{2,1,0:T(8,128)} fusion(bf16[1536,2048]{1,0:T(8,128)(2,1)} %get-tuple-element.7, bf16[1536,768]{0,1:T(8,128)(2,1)} %bitcast.18), kind=kOutput, calls=%fused_computation.6 | convolution fusion | flops 2420637696 | bytes 11796480 | tf_op jit(solution)/shard_map/dot_general | solution.py:22
  180.1 0.0 reduce-scatter.5.cloned.1.call-update
  180.1 0.2 reduce-scatter.3.cloned.1.call-start
  180.3 7.5 %multiply_reduce_fusion = (bf16[1536]{0:T(1024)(128)(2,1)S(1)}, bf16[1536,384]{0,1:T(8,128)(2,1)S(1)}, bf16[1536,384]{0,1:T(8,128)(2,1)S(1)}) fusion(bf16[1536,768]{0,1:T(8,128)(2,1)} %bitcast.19, bf16[1536,2048]{1,0:T(8,128)(2,1)} %get-tuple-element.7, bf16[1,384,2048]{2,1,0:T(8,128)(2,1)} %param.13), kind=kOutput, calls=%fused_computation.17 | convolution fusion | flops 2426534400 | bytes 12585984 | tf_op jit(solution)/shard_map/dot_general | solution.py:22
  187.9 0.0 copy-start.3
  187.9 1.0 copy-done.3
  188.9 0.4 copy-done.4
  189.3 10.6 %convolution_bitcast_fusion = f32[1,2048,768]{2,1,0:T(8,128)} fusion(bf16[1536,2048]{1,0:T(8,128)(2,1)} %get-tuple-element.9, bf16[1536,384]{0,1:T(8,128)(2,1)S(1)} %get-tuple-element.11, bf16[1536,384]{0,1:T(8,128)(2,1)S(1)} %get-tuple-element.12), kind=kOutput, calls=%fused_computation.1 | convolution fusion | flops 4836556800 | bytes 14942208 | tf_op jit(solution)/shard_map/dot_general | solution.py:22
  199.9 0.0 reduce-scatter.3.cloned.1.call-update
  199.9 0.7 convert_element_type.60
  200.7 6.1 %all-to-all-start = ((bf16[64,1,24]{2,1,0:T(2,128)(2,1)}), bf16[64,1,24]{2,1,0:T(2,128)(2,1)S(1)}, u32[]{:S(2)}, u32[]{:S(2)}) async-start(bf16[64,1,24]{2,1,0:T(2,128)(2,1)} %convert_element_type.60), calls=%async_computation | async-start | bytes 65536 | tf_op jit(solution)/shard_map/all_to_all | solution.py:365
  206.9 8.7 %convolution_convert_fusion.rows_ref = bf16[1536,2048]{1,0:T(8,128)(2,1)} fusion(bf16[1,2048,768]{2,1,0:T(8,128)(2,1)S(1)} %copy-done, bf16[1536,384]{0,1:T(8,128)(2,1)} %copy-done.3, bf16[1536,384]{0,1:T(8,128)(2,1)} %copy-done.4), kind=kOutput, calls=%fused_computation | convolution fusion | flops 4839702528 | bytes 11796480 | tf_op jit(solution)/shard_map/dot_general | solution.py:22
  215.6 0.1 fusion.15
  215.7 85.4 %combine.1 = bf16[128,2048]{1,0:T(8,128)(2,1)} custom-call(bf16[1536,2048]{1,0:T(8,128)(2,1)} %convolution_convert_fusion.rows_ref, bf16[8,384,256]{2,1,0:T(8,128)(2,1)} %get-tuple-element.8.pick_ref), custom_call_target="tpu_custom_call" | custom-call | tf_op jit(solution)/shard_map/combine/pallas_call | solution.py:323
  301.1 0.0 all-to-all-done
  301.2 0.3 select_reduce_fusion
  301.5 0.6 divide_convert_fusion
  302.1 1.9 copy.32
  (11 shorter events, 0.1 us)
Async XLA Ops:
  7.2 199.7 %copy-start = (bf16[1,2048,768]{2,1,0:T(8,128)(2,1)S(1)}, bf16[1,2048,768]{2,1,0:T(8,128)(2,1)}, u32[]{:S(2)}) copy-start(bf16[1,2048,768]{2,1,0:T(8,128)(2,1)} %param.12) | copy-start | bytes 9437188
  7.2 294.9 %reduce-scatter.5.cloned.1.call-start = ((), (), s32[]{:S(2)}) async-start(), calls=%async_computation.4 | async-start | bytes 3932160 | tf_op jit(solution)/shard_map/reduce_scatter | solution.py:361
  180.1 122.0 %reduce-scatter.3.cloned.1.call-start = ((), (), s32[]{:S(2)}) async-start(), calls=%async_computation.3 | async-start | bytes 7864320 | tf_op jit(solution)/shard_map/reduce_scatter | solution.py:362
  187.9 1.0 copy-start.3
  187.9 1.4 copy-start.4
  199.9 6.9 %copy-start.1 = (s32[128,8]{0,1:T(8,128)S(1)}, s32[128,8]{0,1:T(8,128)}, u32[]{:S(2)}) copy-start(s32[128,8]{0,1:T(8,128)} %param.9) | copy-start | bytes 12292
  200.7 100.5 %all-to-all-start = ((bf16[64,1,24]{2,1,0:T(2,128)(2,1)}), bf16[64,1,24]{2,1,0:T(2,128)(2,1)S(1)}, u32[]{:S(2)}, u32[]{:S(2)}) async-start(bf16[64,1,24]{2,1,0:T(2,128)(2,1)} %convert_element_type.60), calls=%async_computation | async-start | bytes 65536 | tf_op jit(solution)/shard_map/all_to_all | solution.py:365
  215.7 85.8 %copy-start.2 = (bf16[128,8]{0,1:T(8,128)(2,1)S(1)}, bf16[128,8]{0,1:T(8,128)(2,1)}, u32[]{:S(2)}) copy-start(bf16[128,8]{0,1:T(8,128)(2,1)} %param.10) | copy-start | bytes 6148
Sparse Core Ops, SparseCore 0:
  180.2 37.4 reduce-scatter.4
  220.8 66.2 reduce-scatter.2

commit v2 on v1

--- a/solution.py
+++ b/solution.py
@@ -16,6 +16,8 @@
 ROWS = PEERS * SEG
 YROWS = NZ * SEG
 SLOTS = NY * YROWS
+WIDE = HALF + 128
+SHARE = D // NX
 
 
 def contract(left_side, right_side, left_dim, right_dim):
@@ -40,7 +42,10 @@
                 )
     for dz in (1, NZ - 1):
         pl.semaphore_signal(barrier, inc=1, device_id={"z": (z + dz) % NZ}, device_id_type=MESH)
-    pl.semaphore_wait(barrier, PEERS - 1 + 2)
+    x = lax.axis_index("dp")
+    for dx in range(1, NX):
+        pl.semaphore_signal(barrier, inc=1, device_id={"dp": (x + dx) % NX}, device_id_type=MESH)
+    pl.semaphore_wait(barrier, PEERS - 1 + 2 + NX - 1)
 
 
 def remote(src, dst, send_sem, recv_sem, where):
@@ -54,48 +59,50 @@
 
 
 def table(ids, gates, c):
-    lane = lax.broadcasted_iota(jnp.int32, (TOK, 128), 1)
-    expert = ((lane // 2) % NY) * (NZ * NC) + (lane // 16) * NC + lane % 2
-    second = (lane // 8) % 2
-    named = jnp.zeros((TOK, 128), jnp.float32)
-    weight = jnp.zeros((TOK, 128), jnp.float32)
+    row = lax.broadcasted_iota(jnp.int32, (128, TOK), 0)
+    expert = ((row // 2) % NY) * (NZ * NC) + (row // 16) * NC + row % 2
+    named = jnp.zeros((128, TOK), jnp.float32)
+    weight = jnp.zeros((128, TOK), jnp.float32)
     for k in range(TOPK):
-        hit = ids[:, k : k + 1] == expert
+        hit = ids[k : k + 1, :] == expert
         named += jnp.where(hit, 1.0, 0.0)
-        weight += jnp.where(hit, gates[:, k : k + 1], 0.0)
-    named = named.astype(jnp.bfloat16)
-    weight = weight.astype(jnp.bfloat16)
-    row = lax.broadcasted_iota(jnp.int32, (TOK, TOK), 0)
-    col = lax.broadcasted_iota(jnp.int32, (TOK, TOK), 1)
-    before = jnp.where(row < col, 1.0, 0.0).astype(jnp.bfloat16)
-    same = jnp.where(row == col, 1.0, 0.0).astype(jnp.bfloat16)
-    rank_t = contract(named, before, 0, 0)
-    named_t = contract(named, same, 0, 0)
-    weight_t = contract(weight, same, 0, 0)
-    rank_t = jnp.where(named_t > 0.5, rank_t + (c * CAP).astype(jnp.float32), -1.0)
-    second_t = (lax.broadcasted_iota(jnp.int32, (128, TOK), 0) // 8) % 2
-    return jnp.where(second_t == 1, weight_t, rank_t).astype(jnp.bfloat16)
+        weight += jnp.where(hit, gates[k : k + 1, :], 0.0)
+    first = lax.broadcasted_iota(jnp.int32, (TOK, TOK), 0)
+    second = lax.broadcasted_iota(jnp.int32, (TOK, TOK), 1)
+    before = jnp.where(first < second, 1.0, 0.0).astype(jnp.bfloat16)
+    rank = contract(named.astype(jnp.bfloat16), before, 1, 0) + (c * CAP).astype(jnp.float32)
+    return jnp.where((row // 8) % 2 == 1, weight, jnp.where(named > 0.5, rank, -1.0)).astype(jnp.bfloat16)
 
 
 def dispatch_kernel(
-    ids_ref, gates_ref, d_ref, t_ref, gd_out, tok_out, pick_ref,
-    meta, blocks, staged, scaled, load_sem, pair_send, pair_recv, ring_send, ring_recv, out_send, out_recv,
+    ids_ref, gates_ref, d_ref, t_ref, saved_hbm, gate_up_hbm, down_hbm,
+    tok_out, pick_ref, both_out, route_out, lane_out, down_out,
+    meta, blocks, staged, scaled, gd_rows, saved, w_gate_up, w_down, active, both, route, lanes,
+    down_own, down_going, down_coming,
+    load_sem, pair_send, pair_recv, ring_send, ring_recv, out_send, out_recv, weight_sem, store_sem, down_send, down_recv,
 ):
     y, z, c = place()
+    x = lax.axis_index("dp")
     partner = {"c": 1 - c}
     up, down = {"z": (z + 1) % NZ}, {"z": (z + NZ - 1) % NZ}
     mine = pl.ds(pl.multiple_of(c * TOK, TOK), TOK)
     my_half = pl.ds(pl.multiple_of(c * HALF, HALF), HALF)
     its_half = pl.ds(pl.multiple_of((1 - c) * HALF, HALF), HALF)
     sources = (d_ref, t_ref)
-    outs = (gd_out, tok_out)
+    outs = (gd_rows, tok_out)
 
     loads = [
         pltpu.make_async_copy(sources[a].at[:, my_half], blocks.at[a, z, mine, :], load_sem.at[a]) for a in range(2)
     ]
     for load in loads:
         load.start()
-    meta[z, c] = table(ids_ref[...], gates_ref[...].astype(jnp.float32), c)
+    weights = [
+        pltpu.make_async_copy(src, dst, weight_sem.at[n])
+        for n, (src, dst) in enumerate(((saved_hbm, saved), (down_hbm, w_down), (gate_up_hbm, w_gate_up)))
+    ]
+    for copy in weights:
+        copy.start()
+    meta[z, c] = table(ids_ref[...], gates_ref[...], c)
     plane_barrier(y, z, c)
     pairs = [
         remote(meta.at[z, c], meta.at[z, c], pair_send.at[2], pair_recv.at[2], partner),
@@ -172,7 +179,63 @@
             send_block(a, (z + NZ - 1 - step) % NZ)
             if step < 3:
                 send_block(a, (z + 1 + step) % NZ)
-    for copy in pairs:
+    for copy in weights:
+        copy.wait()
+    pltpu.make_async_copy(gd_rows, gd_rows, out_recv.at[0]).wait()
+    lane = lax.broadcasted_iota(jnp.int32, (YROWS, 128), 1)
+    my_lane = lane == z * 8 + y * NC + c
+
+    def expert_rows(b, carry):
+        rows = pl.ds(pl.multiple_of(b * YROWS, YROWS), YROWS)
+        gate_input = saved[rows, :FF].astype(jnp.float32)
+        up_input = saved[rows, FF:].astype(jnp.float32)
+        logistic = jax.nn.sigmoid(gate_input)
+        swish = gate_input * logistic
+        activated = swish * up_input
+        hidden_grad = contract(gd_rows[rows, :], w_down[...], 1, 1)
+        gate_dot = jnp.sum(activated * hidden_grad, axis=1, keepdims=True)
+        lanes[rows, :] = jnp.where(my_lane, gate_dot, 0.0).astype(jnp.bfloat16)
+        active[rows, :] = activated.astype(jnp.bfloat16)
+        pre_grad = hidden_grad * up_input * logistic * (1.0 + gate_input * (1.0 - logistic))
+        both[rows, :FF] = pre_grad.astype(jnp.bfloat16)
+        both[rows, FF:] = (hidden_grad * swish).astype(jnp.bfloat16)
+
+        def tile(i, inner):
+            cols = pl.ds(pl.multiple_of(i * 512, 512), 512)
+            route[rows, cols] = contract(both[rows, :], w_gate_up[cols, :], 1, 1).astype(jnp.bfloat16)
+            return inner
+
+        return lax.fori_loop(0, D // 512, tile, carry)
+
+    lax.fori_loop(0, NY, expert_rows, 0)
+    stores = [
+        pltpu.make_async_copy(src, dst, store_sem.at[n])
+        for n, (src, dst) in enumerate(((route, route_out), (both, both_out), (lanes, lane_out)))
+    ]
+    for copy in stores:
+        copy.start()
+
+    def down_part(dx):
+        cols = pl.ds(pl.multiple_of(((x + dx) % NX) * SHARE, SHARE), SHARE)
+        return contract(active[...], gd_rows[:, cols], 0, 0)
+
+    shares = []
+    for dx in (2, 1, 3):
+        down_going[dx - 1] = down_part(dx).astype(jnp.bfloat16)
+        copy = remote(
+            down_going.at[dx - 1], down_coming.at[dx - 1], down_send.at[dx - 1], down_recv.at[dx - 1], {"dp": (x + dx) % NX}
+        )
+        copy.start()
+        shares.append(copy)
+    down_own[...] = down_part(0)
+    for copy in shares:
+        copy.wait_recv()
+    total = down_own[...]
+    for n in range(NX - 1):
+        total += down_coming[n].astype(jnp.float32)
+    down_out[...] = total
+
+    for copy in shares + pairs:
         copy.wait_send()
     for a in range(3):
         for step in range(4):
@@ -181,18 +244,34 @@
     for a in range(2):
         most = staged.at[a, pl.ds(0, PEERS - 1)]
         pltpu.make_async_copy(most, most, out_send.at[a]).wait()
-        pltpu.make_async_copy(outs[a], outs[a], out_recv.at[a]).wait()
+    for copy in stores:
+        copy.wait()
+    pltpu.make_async_copy(tok_out, tok_out, out_recv.at[1]).wait()
 
 
 def combine_kernel(
-    rows_ref, pick_ref, out_ref,
-    arrived, going, coming, last, out_send, out_recv, ring_send, ring_recv, pair_send, pair_recv,
+    rows_ref, lane_ref, pick_ref, tok_hbm, both_hbm, ids_ref, gates_ref, out_ref, gate_ref, share_ref,
+    arrived, going, coming, last, tok, both, share_going, share_coming,
+    out_send, out_recv, lane_send, lane_recv, ring_send, ring_recv, pair_send, pair_recv, load_sem, share_send, share_recv,
 ):
     y, z, c = place()
+    x = lax.axis_index("dp")
     partner = {"c": 1 - c}
     up, down = {"z": (z + 1) % NZ}, {"z": (z + NZ - 1) % NZ}
     my_half = pl.ds(pl.multiple_of(c * HALF, HALF), HALF)
     its_half = pl.ds(pl.multiple_of((1 - c) * HALF, HALF), HALF)
+    loads = [
+        pltpu.make_async_copy(both_hbm, both, load_sem.at[0]),
+        pltpu.make_async_copy(tok_hbm, tok, load_sem.at[1]),
+    ]
+    for load in loads:
+        load.start()
+
+    def clear(n, carry):
+        arrived[n, :, HALF:] = jnp.zeros((ROWS, 128), jnp.bfloat16)
+        return carry
+
+    lax.fori_loop(0, NZ, clear, 0)
     plane_barrier(y, z, c)
     at = pl.ds(pl.multiple_of((y * NC + c) * SEG, SEG), SEG)
     order = (4, 5, 3, 6, 2, 7, 1, 0)
@@ -201,13 +280,17 @@
         for dy in (1, 3, 2, 0):
             for dc in range(NC):
                 py, pc = (y + dy) % NY, (c + dc) % NC
-                src = rows_ref.at[
-                    pl.ds(pl.multiple_of(py * YROWS + block * SEG, SEG), SEG), pl.ds(pl.multiple_of(pc * HALF, HALF), HALF)
-                ]
+                rows = pl.ds(pl.multiple_of(py * YROWS + block * SEG, SEG), SEG)
+                half = (rows_ref.at[rows, pl.ds(pl.multiple_of(pc * HALF, HALF), HALF)], arrived.at[block, at, :HALF])
+                lane = (lane_ref.at[rows, :], arrived.at[block, at, HALF:])
                 if dy or dc:
-                    remote(src, arrived.at[block, at, :], out_send, out_recv.at[n], {"y": py, "c": pc}).start()
+                    remote(*half, out_send, out_recv.at[n], {"y": py, "c": pc}).start()
                 else:
-                    pltpu.make_async_copy(src, arrived.at[block, at, :], out_recv.at[n]).start()
+                    pltpu.make_async_copy(*half, out_recv.at[n]).start()
+                if dy and dc == 0:
+                    remote(*lane, lane_send, lane_recv.at[n], {"y": py, "c": pc}).start()
+                elif dc == 0:
+                    pltpu.make_async_copy(*lane, lane_recv.at[n]).start()
 
     def ring(step, direction):
         rows = pl.ds(direction * TOK, TOK) if step == 0 else pl.ds(0, PAIR)
@@ -220,23 +303,50 @@
         )
 
     def ready(n):
-        block = arrived.at[(z + order[n]) % NZ]
-        pltpu.make_async_copy(block, block, out_recv.at[n]).wait()
+        block = (z + order[n]) % NZ
+        half, lane = arrived.at[block, :, :HALF], arrived.at[block, : ROWS // 2, HALF:]
+        pltpu.make_async_copy(half, half, out_recv.at[n]).wait()
+        pltpu.make_async_copy(lane, lane, lane_recv.at[n]).wait()
 
     def partial(n, add, store):
         block = (z + order[n]) % NZ
 
         def tile(i, carry):
-            cols = pl.ds(pl.multiple_of(i * TILE, TILE), TILE)
+            cols = pl.ds(pl.multiple_of(i * 384, 384), 384)
             store(cols, add(cols, contract(pick_ref[block], arrived[block, :, cols], 0, 0)))
             return carry
 
-        lax.fori_loop(0, HALF // TILE, tile, 0)
+        lax.fori_loop(0, WIDE // 384, tile, 0)
 
     def store_first(cols, value):
         value = value.astype(jnp.bfloat16)
         going[0, 0, :TOK, cols] = value[:TOK]
         going[1, 0, TOK:, cols] = value[TOK:]
+
+    for load in loads:
+        load.wait()
+
+    def share_tiles(dx, store):
+        def tile(i, carry):
+            cols = pl.ds(pl.multiple_of(((x + dx) % NX) * SHARE + i * 256, 256), 256)
+            store(pl.ds(pl.multiple_of(i * 256, 256), 256), contract(tok[:, cols], both[...], 0, 0))
+            return carry
+
+        lax.fori_loop(0, SHARE // 256, tile, 0)
+
+    shares = []
+    for dx in (2, 1, 3):
+
+        def store_going(rows, value):
+            share_going[dx - 1, rows, :] = value.astype(jnp.bfloat16)
+
+        share_tiles(dx, store_going)
+        copy = remote(
+            share_going.at[dx - 1], share_coming.at[dx - 1], share_send.at[dx - 1], share_recv.at[dx - 1],
+            {"dp": (x + dx) % NX},
+        )
+        copy.start()
+        shares.append(copy)
 
     ready(0)
     partial(0, lambda cols, value: value, store_first)
@@ -261,6 +371,14 @@
 
             partial(n, add, store)
             ring(step, direction).start()
+    def store_own(rows, value):
+        share_ref[rows, :] = value
+
+    share_tiles(0, store_own)
+    for copy in shares:
+        copy.wait_recv()
+    for n in range(NX - 1):
+        share_ref[...] += share_coming[n].astype(jnp.float32)
     ready(7)
     for direction in range(2):
         ring(3, direction).wait_recv()
@@ -278,15 +396,28 @@
     its = pl.ds(pl.multiple_of((1 - c) * TOK, TOK), TOK)
     swap = remote(going.at[0, 0, its, :], last, pair_send, pair_recv, partner)
     swap.start()
-    out_ref[:, my_half] = going[0, 0, mine, :]
+    out_ref[:, my_half] = going[0, 0, mine, :HALF]
     swap.wait_recv()
-    out_ref[:, its_half] = last[...]
+    out_ref[:, its_half] = last[:, :HALF]
+    dense = going[0, 0, mine, HALF:] + last[:, HALF:]
+    first = lax.broadcasted_iota(jnp.int32, (TOK, TOK), 0)
+    second = lax.broadcasted_iota(jnp.int32, (TOK, TOK), 1)
+    dense = contract(dense, jnp.where(first == second, 1.0, 0.0).astype(jnp.bfloat16), 0, 0)
+    row = lax.broadcasted_iota(jnp.int32, (128, TOK), 0)
+    expert = ((row // 2) % NY) * (NZ * NC) + (row // 8) * NC + row % 2
+    for k in range(TOPK):
+        hit = ids_ref[k : k + 1, :] == expert
+        picked = jnp.sum(jnp.where(hit, dense, 0.0), axis=0, keepdims=True)
+        gate_ref[k : k + 1, :] = picked / gates_ref[k : k + 1, :]
     swap.wait_send()
+    for copy in shares:
+        copy.wait_send()
     for step in range(1, 4):
         for direction in range(2):
             ring(step, direction).wait_send()
-    most = arrived.at[pl.ds(0, PEERS - 1)]
-    pltpu.make_async_copy(most, most, out_send).wait()
+    half, lane = arrived.at[pl.ds(0, PEERS - 1), :, :HALF], arrived.at[pl.ds(0, NY - 1), :, HALF:]
+    pltpu.make_async_copy(half, half, out_send).wait()
+    pltpu.make_async_copy(lane, lane, lane_send).wait()
 
 
 ANY = pl.BlockSpec(memory_space=pl.ANY)
@@ -294,18 +425,35 @@
 DMA = pltpu.SemaphoreType.DMA
 
 
-def dispatch(expert_ids, gate_weights, d_output, tokens):
-    rows = jax.ShapeDtypeStruct((SLOTS, D), jnp.bfloat16)
+def bf16(*shape):
+    return jax.ShapeDtypeStruct(shape, jnp.bfloat16)
+
+
+def dispatch(ids, gates, d_output, tokens, saved, w_gate_up, w_down):
     return pl.pallas_call(
         dispatch_kernel,
-        out_shape=(rows, rows, jax.ShapeDtypeStruct((NZ, ROWS, PAIR), jnp.bfloat16)),
-        in_specs=[VMEM, VMEM, ANY, ANY],
-        out_specs=(ANY, ANY, VMEM),
+        out_shape=(
+            bf16(SLOTS, D), bf16(NZ, ROWS, PAIR), bf16(SLOTS, 2 * FF), bf16(SLOTS, D), bf16(SLOTS, 128),
+            jax.ShapeDtypeStruct((FF, SHARE), jnp.float32),
+        ),
+        in_specs=[VMEM, VMEM, ANY, ANY, ANY, ANY, ANY],
+        out_specs=(ANY, VMEM, ANY, ANY, ANY, VMEM),
         scratch_shapes=[
             pltpu.VMEM((NZ, NC, 128, TOK), jnp.bfloat16),
             pltpu.VMEM((2, NZ, PAIR, HALF), jnp.bfloat16),
             pltpu.VMEM((2, NZ, ROWS, HALF), jnp.bfloat16),
             pltpu.VMEM((ROWS, PAIR), jnp.bfloat16),
+            pltpu.VMEM((SLOTS, D), jnp.bfloat16),
+            pltpu.VMEM((SLOTS, 2 * FF), jnp.bfloat16),
+            pltpu.VMEM((D, 2 * FF), jnp.bfloat16),
+            pltpu.VMEM((FF, D), jnp.bfloat16),
+            pltpu.VMEM((SLOTS, FF), jnp.bfloat16),
+            pltpu.VMEM((SLOTS, 2 * FF), jnp.bfloat16),
+            pltpu.VMEM((SLOTS, D), jnp.bfloat16),
+            pltpu.VMEM((SLOTS, 128), jnp.bfloat16),
+            pltpu.VMEM((FF, SHARE), jnp.float32),
+            pltpu.VMEM((NX - 1, FF, SHARE), jnp.bfloat16),
+            pltpu.VMEM((NX - 1, FF, SHARE), jnp.bfloat16),
             DMA((2,)),
             DMA((3,)),
             DMA((3,)),
@@ -313,71 +461,58 @@
             DMA((3, 4, 2)),
             DMA((2,)),
             DMA((2,)),
+            DMA((3,)),
+            DMA((3,)),
+            DMA((NX - 1,)),
+            DMA((NX - 1,)),
         ],
-        compiler_params=pltpu.CompilerParams(collective_id=0, has_side_effects=True),
+        compiler_params=pltpu.CompilerParams(collective_id=0, has_side_effects=True, vmem_limit_bytes=63 << 20),
         name="dispatch",
-    )(expert_ids, gate_weights, d_output, tokens)
-
-
-def combine(route_rows, pick):
+    )(ids, gates, d_output, tokens, saved, w_gate_up, w_down)
+
+
+def combine(route_rows, lanes, pick, input_rows, both_grad, ids, gates):
     return pl.pallas_call(
         combine_kernel,
-        out_shape=jax.ShapeDtypeStruct((TOK, D), jnp.bfloat16),
-        in_specs=[ANY, VMEM],
-        out_specs=VMEM,
+        out_shape=(
+            bf16(TOK, D), jax.ShapeDtypeStruct((TOPK, TOK), jnp.float32),
+            jax.ShapeDtypeStruct((SHARE, 2 * FF), jnp.float32),
+        ),
+        in_specs=[ANY, ANY, VMEM, ANY, ANY, VMEM, VMEM],
+        out_specs=(VMEM, VMEM, VMEM),
         scratch_shapes=[
-            pltpu.VMEM((NZ, ROWS, HALF), jnp.bfloat16),
-            pltpu.VMEM((2, 4, PAIR, HALF), jnp.bfloat16),
-            pltpu.VMEM((2, 4, PAIR, HALF), jnp.bfloat16),
-            pltpu.VMEM((TOK, HALF), jnp.bfloat16),
+            pltpu.VMEM((NZ, ROWS, WIDE), jnp.bfloat16),
+            pltpu.VMEM((2, 4, PAIR, WIDE), jnp.bfloat16),
+            pltpu.VMEM((2, 4, PAIR, WIDE), jnp.bfloat16),
+            pltpu.VMEM((TOK, WIDE), jnp.bfloat16),
+            pltpu.VMEM((SLOTS, D), jnp.bfloat16),
+            pltpu.VMEM((SLOTS, 2 * FF), jnp.bfloat16),
+            pltpu.VMEM((NX - 1, SHARE, 2 * FF), jnp.bfloat16),
+            pltpu.VMEM((NX - 1, SHARE, 2 * FF), jnp.bfloat16),
+            DMA,
+            DMA((8,)),
             DMA,
             DMA((8,)),
             DMA((2, 4)),
             DMA((2, 4)),
             DMA,
             DMA,
+            DMA((2,)),
+            DMA((NX - 1,)),
+            DMA((NX - 1,)),
         ],
-        compiler_params=pltpu.CompilerParams(collective_id=1, has_side_effects=True),
+        compiler_params=pltpu.CompilerParams(collective_id=1, has_side_effects=True, vmem_limit_bytes=63 << 20),
         name="combine",
-    )(route_rows, pick)
+    )(route_rows, lanes, pick, input_rows, both_grad, ids, gates)
 
 
 def on_device(tokens, d_output, expert_ids, gate_weights, pre_acts, w_gate_up, w_down):
-    grad_rows, input_rows, pick = dispatch(expert_ids, gate_weights, d_output, tokens)
-    saved = pre_acts[0, 0]
-    gate_input = saved[:, :FF].astype(jnp.float32)
-    up_input = saved[:, FF:].astype(jnp.float32)
-    logistic = jax.nn.sigmoid(gate_input)
-    swish = gate_input * logistic
-    activated = swish * up_input
-    hidden_grad = contract(grad_rows, w_down[0], 1, 1)
-    gate_dot = jnp.sum(activated * hidden_grad, axis=1).astype(jnp.bfloat16)
-    up_grad = hidden_grad * swish
-    pre_grad = hidden_grad * up_input * logistic * (1.0 + gate_input * (1.0 - logistic))
-    both_grad = jnp.concatenate([pre_grad, up_grad], axis=1).astype(jnp.bfloat16)
-    route_grad = contract(both_grad, w_gate_up[0], 1, 1).astype(jnp.bfloat16)
-    down_grad = contract(activated.astype(jnp.bfloat16), grad_rows, 0, 0)
-    gate_up_grad = contract(input_rows, both_grad, 0, 0)
-    down_share = lax.psum_scatter(down_grad[None], "dp", scatter_dimension=2, tiled=True)
-    gate_up_share = lax.psum_scatter(gate_up_grad[None], "dp", scatter_dimension=1, tiled=True)
-    token_grads = combine(route_grad, pick)
-
-    home = lax.all_to_all(
-        gate_dot.reshape(NY * NZ * NC, 1, CAP), ("y", "z", "c"), split_axis=0, concat_axis=0, tiled=True
-    ).reshape(NY * NZ * NC, CAP)
-    experts = jnp.arange(NY * NZ * NC, dtype=jnp.int32)
-    hit = (expert_ids[:, :, None] == experts).astype(jnp.bfloat16)
-    named = jnp.sum(hit, axis=1)
-    order = jnp.arange(TOK, dtype=jnp.int32)
-    before = (order[:, None] > order[None, :]).astype(jnp.bfloat16)
-    rank = contract(before, named, 1, 0)
-    slots = jnp.arange(CAP, dtype=jnp.float32)
-    dense = jnp.sum(
-        jnp.where(rank[:, :, None] == slots, home.astype(jnp.float32)[None], 0.0), axis=2
+    ids, gates = expert_ids.T, gate_weights.T.astype(jnp.float32)
+    input_rows, pick, both_grad, route_grad, lanes, down_share = dispatch(
+        ids, gates, d_output, tokens, pre_acts[0, 0], w_gate_up[0], w_down[0]
     )
-    picked = jnp.sum(jnp.where(expert_ids[:, :, None] == experts, dense[:, None, :], 0.0), axis=2)
-    gate_grads = (picked / gate_weights.astype(jnp.float32)).astype(jnp.bfloat16)
-    return token_grads, gate_grads, gate_up_share, down_share
+    token_grads, gate_grads, gate_up_share = combine(route_grad, lanes, pick, input_rows, both_grad, ids, gates)
+    return token_grads, gate_grads.T.astype(jnp.bfloat16), gate_up_share[None], down_share[None]
 
 
 def solution(mesh):

time: 311 us -> 257 us (0.83)
  matrix products: 35 us -> 0 us
  between operations: 14.2 us -> 0.66 us
  starting transfers between devices: 6.39 us -> 0 us
  local copies, waits for them, and re-layouts: 11.3 us -> 5.41 us
  Pallas kernels: 243 us -> 248 us
    dot_general x5 -> x0, matrix products: 35 us -> none  [contract(): lax.dot_general(left_side, right_side, (((left_dim,), (right_dim,)), ((),...]
    all_to_all x1 -> x0, starting transfers between devices: 6.13 us -> none  [on_device(): lax.all_to_all(gate_dot.reshape(NY * NZ * NC, 1, CAP), ('y', 'z', 'c'), s...]
    pallas_call x2, Pallas kernels: 243 us -> 248 us  [the longest x1 159 us: dispatch(): pl.pallas_call(dispatch_kernel, out_shape=(bf16(SLOTS, D), bf16(NZ, ROWS,...]
    unnamed x14 -> x5, local copies, waits for them, and re-layouts: 10.5 us -> 5.41 us
  transfers between devices with their start and end apart: 3 -> 0, of which waited for: 0 -> 0; matrix products, arithmetic and copies ran while one was open for 9% -> 0% of each run, Pallas kernels for 27% -> 0%
where the time goes in v2:
time: 257 us
  Pallas kernels  248 us (96%)
  local copies, waits for them, and re-layouts  5.41 us (2%)
  other arithmetic  2.61 us (1%)
    pallas_call x1, Pallas kernels, dispatch(): pl.pallas_call(dispatch_kernel, out_shape=(bf16(SLOTS, D), bf16(NZ, ROWS,...  159 us
    pallas_call x1, Pallas kernels, combine(): pl.pallas_call(combine_kernel, out_shape=(bf16(TOK, D), jax.ShapeDtypeStr...  89.4 us
    unnamed x5, local copies, waits for them, and re-layouts  5.41 us

profile of v2, /device:TPU:1, one launch (start us, length us, event | category | flops | bytes accessed | tf_op | source)
XLA Modules:
  0.0 257.1 jit_solution(780115305287633835)
XLA Ops:
  0.6 1.3 convert_bitcast_fusion.gates_ref
  1.9 159.1 %dispatch.1 = (bf16[1536,2048]{1,0:T(8,128)(2,1)}, bf16[8,384,256]{2,1,0:T(8,128)(2,1)}, bf16[1536,768]{1,0:T(8,128)(2,1)}, bf16[1536,2048]{1,0:T(8,128)(2,1)}, ...) custom-call(s32[8,128]{1,0:T(8,128)} %bitcast.15, f32[8,128]{1,0:T(8,128)} %convert_bitcast_fusion.gates_ref, ...), custom_call_target="tpu_custom_call" | custom-call | tf_op jit(solution)/shard_map/dispatch/pallas_call | solution.py:433
  161.0 89.4 %combine.1 = (bf16[128,2048]{1,0:T(8,128)(2,1)}, f32[8,128]{1,0:T(8,128)}, f32[512,768]{1,0:T(8,128)}) custom-call(bf16[1536,2048]{1,0:T(8,128)(2,1)} %get-tuple-element.13.rows_ref, bf16[1536,128]{1,0:T(8,128)(2,1)} %get-tuple-element.14.lane_ref, bf16[8,384,256]{2,1,0:T(8,128)(2,1)} %get-tuple-element.15.pick_ref, ...), custom_call_target="tpu_custom_call" | custom-call | tf_op jit(solution)/shard_map/combine/pallas_call | solution.py:475
  250.4 0.0 copy-start
  250.4 1.3 convert_bitcast_fusion.1
  251.7 1.9 copy.14
  253.6 2.7 %copy.15 = f32[1,512,768]{2,1,0:T(8,128)} copy(f32[1,512,768]{2,1,0:T(8,128)} %bitcast.13) | data formatting | bytes 3145728
  256.3 0.0 copy-done
  256.3 0.9 copy.16
Async XLA Ops:
  250.4 5.9 %copy-start = (f32[384,512]{1,0:T(8,128)S(1)}, f32[384,512]{1,0:T(8,128)}, u32[]{:S(2)}) copy-start(f32[384,512]{1,0:T(8,128)} %get-tuple-element.21) | copy-start | bytes 2359300

commit v3 on v2

v3 whole, which is shorter than its diff:
```python
import jax
import jax.numpy as jnp
from jax import lax
from jax.experimental import pallas as pl
from jax.experimental.pallas import tpu as pltpu
from jax.sharding import Mesh, PartitionSpec as P

MESH = pl.DeviceIdType.MESH
NY, NZ, NC, NX = 4, 8, 2, 4
TOK, TOPK, D, FF, CAP = 128, 8, 2048, 384, 24
HALF = D // 2
TILE = min(256, HALF)
PAIR = 2 * TOK
SEG = 2 * CAP
PEERS = NY * NC
ROWS = PEERS * SEG
YROWS = NZ * SEG
SLOTS = NY * YROWS
SHARE = D // NX


def contract(left_side, right_side, left_dim, right_dim):
    return lax.dot_general(
        left_side,
        right_side,
        (((left_dim,), (right_dim,)), ((), ())),
        preferred_element_type=jnp.float32,
    )


def plane_barrier(y, z, c):
    barrier = pltpu.get_barrier_semaphore()
    for dy in range(NY):
        for dc in range(NC):
            if dy or dc:
                pl.semaphore_signal(
                    barrier,
                    inc=1,
                    device_id={"y": (y + dy) % NY, "c": (c + dc) % NC},
                    device_id_type=MESH,
                )
    for dz in (1, NZ - 1):
        pl.semaphore_signal(barrier, inc=1, device_id={"z": (z + dz) % NZ}, device_id_type=MESH)
    x = lax.axis_index("dp")
    for dx in range(1, NX):
        pl.semaphore_signal(barrier, inc=1, device_id={"dp": (x + dx) % NX}, device_id_type=MESH)
    pl.semaphore_wait(barrier, PEERS - 1 + 2 + NX - 1)


def remote(src, dst, send_sem, recv_sem, where):
    return pltpu.make_async_remote_copy(
        src_ref=src, dst_ref=dst, send_sem=send_sem, recv_sem=recv_sem, device_id=where, device_id_type=MESH
    )


def place():
    return lax.axis_index("y"), lax.axis_index("z"), lax.axis_index("c")


def table(ids, gates, c):
    row = lax.broadcasted_iota(jnp.int32, (128, TOK), 0)
    expert = ((row // 2) % NY) * (NZ * NC) + (row // 16) * NC + row % 2
    named = jnp.zeros((128, TOK), jnp.float32)
    weight = jnp.zeros((128, TOK), jnp.float32)
    for k in range(TOPK):
        hit = ids[k : k + 1, :] == expert
        named += jnp.where(hit, 1.0, 0.0)
        weight += jnp.where(hit, gates[k : k + 1, :], 0.0)
    first = lax.broadcasted_iota(jnp.int32, (TOK, TOK), 0)
    second = lax.broadcasted_iota(jnp.int32, (TOK, TOK), 1)
    before = jnp.where(first < second, 1.0, 0.0).astype(jnp.bfloat16)
    rank = contract(named.astype(jnp.bfloat16), before, 1, 0) + (c * CAP).astype(jnp.float32)
    return jnp.where((row // 8) % 2 == 1, weight, jnp.where(named > 0.5, rank, -1.0)).astype(jnp.bfloat16)


def layer_kernel(
    ids_ref, gates_ref, d_ref, t_ref, saved_hbm, gate_up_hbm, down_hbm,
    tok_out, out_ref, gate_ref, share_ref, down_out,
    meta, blocks, staged, scaled, pick_ref, gd_rows, saved, w_gate_up, w_down, active, both, route, lanes,
    down_own, down_going, down_coming, arrived, arrived_lane, coming, coming_lane, going_lane, last, last_lane, share_coming,
    load_sem, pair_send, pair_recv, ring_send, ring_recv, out_send, out_recv, own_sem, weight_sem, down_send, down_recv,
    back_send, back_recv, lane_send, lane_recv, sum_send, sum_recv, sum_lane_send, sum_lane_recv,
    swap_send, swap_recv, tok_sem, share_send, share_recv,
):
    y, z, c = place()
    x = lax.axis_index("dp")
    partner = {"c": 1 - c}
    up, down = {"z": (z + 1) % NZ}, {"z": (z + NZ - 1) % NZ}
    mine = pl.ds(pl.multiple_of(c * TOK, TOK), TOK)
    my_half = pl.ds(pl.multiple_of(c * HALF, HALF), HALF)
    its_half = pl.ds(pl.multiple_of((1 - c) * HALF, HALF), HALF)
    sources = (d_ref, t_ref)
    outs = (gd_rows, tok_out)

    loads = [
        pltpu.make_async_copy(sources[a].at[:, my_half], blocks.at[a, z, mine, :], load_sem.at[a]) for a in range(2)
    ]
    for load in loads:
        load.start()
    weights = [
        pltpu.make_async_copy(src, dst, weight_sem.at[n])
        for n, (src, dst) in enumerate(((saved_hbm, saved), (down_hbm, w_down), (gate_up_hbm, w_gate_up)))
    ]
    for copy in weights:
        copy.start()
    arrived_lane[...] = jnp.zeros_like(arrived_lane)
    meta[z, c] = table(ids_ref[...], gates_ref[...], c)
    plane_barrier(y, z, c)
    pairs = [
        remote(meta.at[z, c], meta.at[z, c], pair_send.at[2], pair_recv.at[2], partner),
        remote(sources[0].at[:, its_half], blocks.at[0, z, mine, :], pair_send.at[0], pair_recv.at[0], partner),
        remote(sources[1].at[:, its_half], blocks.at[1, z, mine, :], pair_send.at[1], pair_recv.at[1], partner),
    ]
    for copy in pairs:
        copy.start()

    def ring(a, step, direction):
        where = up if direction == 0 else down
        block = (z + NZ - step) % NZ if direction == 0 else (z + step) % NZ
        if a == 2:
            ref = meta.at[block, direction] if step == 3 else meta.at[block]
        else:
            ref = blocks.at[a, block, pl.ds(direction * TOK, TOK), :] if step == 3 else blocks.at[a, block]
        return remote(ref, ref, ring_send.at[a, step, direction], ring_recv.at[a, step, direction], where)

    def pick_block(block):
        rows = jnp.concatenate(
            [meta[block, i, pl.ds(pl.multiple_of(z * 16, 16), 16), :].astype(jnp.float32) for i in range(2)], axis=1
        )
        rank, weight = rows[:8, :], rows[8:, :]
        slot = lax.broadcasted_iota(jnp.int32, (PEERS, SEG, PAIR), 1).astype(jnp.float32)
        hit = jnp.where(rank[:, None, :] == slot, 1.0, 0.0)
        pick_ref[block] = hit.reshape(ROWS, PAIR).astype(jnp.bfloat16)
        scaled[...] = (hit * weight[:, None, :]).reshape(ROWS, PAIR).astype(jnp.bfloat16)

    def sent(a, n):
        most, own = staged.at[n, : ROWS - SEG], staged.at[n, :SEG]
        pltpu.make_async_copy(most, most, out_send.at[a, n]).wait()
        pltpu.make_async_copy(own, own, own_sem.at[a, n]).wait()

    def send_block(a, n, block):
        if a == 0:
            pick_block(block)
        else:
            sent(0, n)

        def tile(i, carry):
            cols = pl.ds(pl.multiple_of(i * TILE, TILE), TILE)
            matrix = scaled[...] if a == 0 else pick_ref[block]
            staged[n, :, cols] = contract(matrix, blocks[a, block, :, cols], 1, 0).astype(jnp.bfloat16)
            return carry

        lax.fori_loop(0, HALF // TILE, tile, 0)
        at = outs[a].at[pl.ds(pl.multiple_of(y * YROWS + block * SEG, SEG), SEG), my_half]
        for dy in (1, 3, 2, 0):
            for dc in range(NC):
                py, pc = (y + dy) % NY, (c + dc) % NC
                src = staged.at[n, pl.ds(pl.multiple_of((py * NC + pc) * SEG, SEG), SEG), :]
                if dy or dc:
                    remote(src, at, out_send.at[a, n], out_recv.at[a], {"y": py, "c": pc}).start()
                else:
                    pltpu.make_async_copy(src, at, own_sem.at[a, n]).start()

    def begin(a):
        loads[a].wait()
        pairs[a + 1].wait_recv()
        for direction in range(2):
            ring(a, 0, direction).start()

    pairs[0].wait_recv()
    for direction in range(2):
        ring(2, 0, direction).start()
    begin(0)
    for a in range(2):
        send_block(a, 0, z)
        for step in range(4):
            for direction in range(2):
                if a == 0:
                    ring(2, step, direction).wait_recv()
                ring(a, step, direction).wait_recv()
            if step < 3:
                for direction in range(2):
                    if a == 0:
                        ring(2, step + 1, direction).start()
                    ring(a, step + 1, direction).start()
            elif a == 0:
                begin(1)
            send_block(a, 2 * step + 1, (z + NZ - 1 - step) % NZ)
            if step < 3:
                send_block(a, 2 * step + 2, (z + 1 + step) % NZ)
    for copy in weights:
        copy.wait()
    others = staged.at[: NZ - 1]
    pltpu.make_async_copy(others, others, out_recv.at[0]).wait()
    lane = lax.broadcasted_iota(jnp.int32, (YROWS, 128), 1)
    my_lane = lane == z * 8 + y * NC + c

    def expert_rows(b, carry):
        rows = pl.ds(pl.multiple_of(b * YROWS, YROWS), YROWS)
        gate_input = saved[rows, :FF].astype(jnp.float32)
        up_input = saved[rows, FF:].astype(jnp.float32)
        logistic = jax.nn.sigmoid(gate_input)
        swish = gate_input * logistic
        activated = swish * up_input
        hidden_grad = contract(gd_rows[rows, :], w_down[...], 1, 1)
        gate_dot = jnp.sum(activated * hidden_grad, axis=1, keepdims=True)
        lanes[rows, :] = jnp.where(my_lane, gate_dot, 0.0).astype(jnp.bfloat16)
        active[rows, :] = activated.astype(jnp.bfloat16)
        pre_grad = hidden_grad * up_input * logistic * (1.0 + gate_input * (1.0 - logistic))
        both[rows, :FF] = pre_grad.astype(jnp.bfloat16)
        both[rows, FF:] = (hidden_grad * swish).astype(jnp.bfloat16)

        def tile(i, inner):
            cols = pl.ds(pl.multiple_of(i * 512, 512), 512)
            route[rows, cols] = contract(both[rows, :], w_gate_up[cols, :], 1, 1).astype(jnp.bfloat16)
            return inner

        return lax.fori_loop(0, D // 512, tile, carry)

    lax.fori_loop(0, NY, expert_rows, 0)
    at = pl.ds(pl.multiple_of((y * NC + c) * SEG, SEG), SEG)
    order = (4, 5, 3, 6, 2, 7, 1, 0)
    for n, dz in enumerate(order):
        block = (z + dz) % NZ
        for dy in (1, 3, 2, 0):
            for dc in range(NC):
                py, pc = (y + dy) % NY, (c + dc) % NC
                rows = pl.ds(pl.multiple_of(py * YROWS + block * SEG, SEG), SEG)
                half = (route.at[rows, pl.ds(pl.multiple_of(pc * HALF, HALF), HALF)], arrived.at[block, at, :])
                lane = (lanes.at[rows, :], arrived_lane.at[block, at, :])
                if dy or dc:
                    remote(*half, back_send, back_recv.at[n], {"y": py, "c": pc}).start()
                else:
                    pltpu.make_async_copy(*half, back_recv.at[n]).start()
                if dy and dc == 0:
                    remote(*lane, lane_send, lane_recv.at[n], {"y": py, "c": pc}).start()
                elif dc == 0:
                    pltpu.make_async_copy(*lane, lane_recv.at[n]).start()

    def down_part(dx):
        cols = pl.ds(pl.multiple_of(((x + dx) % NX) * SHARE, SHARE), SHARE)
        return contract(active[...], gd_rows[:, cols], 0, 0)

    shares = []
    for dx in (2, 1, 3):
        down_going[dx - 1] = down_part(dx).astype(jnp.bfloat16)
        copy = remote(
            down_going.at[dx - 1], down_coming.at[dx - 1], down_send.at[dx - 1], down_recv.at[dx - 1], {"dp": (x + dx) % NX}
        )
        copy.start()
        shares.append(copy)
    down_own[...] = down_part(0)
    for copy in shares:
        copy.wait_recv()
    total = down_own[...]
    for n in range(NX - 1):
        total += down_coming[n].astype(jnp.float32)
    down_out[...] = total

    for step in range(4):
        for direction in range(2):
            ring(0, step, direction).wait_send()

    def going(direction, step):
        return blocks.at[0, direction * 4 + step]

    def chain(step, direction):
        rows = pl.ds(direction * TOK, TOK) if step == 0 else pl.ds(0, PAIR)
        where = up if direction == 0 else down
        return (
            remote(
                going(direction, step).at[rows, :], coming.at[direction, step, rows, :],
                sum_send.at[direction, step], sum_recv.at[direction, step], where,
            ),
            remote(
                going_lane.at[direction, step, rows, :], coming_lane.at[direction, step, rows, :],
                sum_lane_send.at[direction, step], sum_lane_recv.at[direction, step], where,
            ),
        )

    def chain_start(step, direction):
        for copy in chain(step, direction):
            copy.start()

    def chain_recv(step, direction):
        for copy in chain(step, direction):
            copy.wait_recv()

    def chain_sent(step, direction):
        for copy in chain(step, direction):
            copy.wait_send()

    def ready(n):
        block = (z + order[n]) % NZ
        half, lane = arrived.at[block], arrived_lane.at[block, : ROWS // 2]
        pltpu.make_async_copy(half, half, back_recv.at[n]).wait()
        pltpu.make_async_copy(lane, lane, lane_recv.at[n]).wait()

    def partial(n, step, directions, keep):
        block = (z + order[n]) % NZ

        def part(came, rows):
            value = contract(pick_ref[block], rows, 0, 0)
            for direction in directions:
                if step == 1:
                    first = came(direction, 0, pl.ds(direction * TOK, TOK)).astype(jnp.float32)
                    if direction == 0:
                        value = jnp.concatenate([value[:TOK] + first, value[TOK:]], axis=0)
                    else:
                        value = jnp.concatenate([value[:TOK], value[TOK:] + first], axis=0)
                elif step > 1:
                    value = value + came(direction, step - 1, pl.ds(0, PAIR)).astype(jnp.float32)
            return value.astype(jnp.bfloat16)

        def tile(i, carry):
            cols = pl.ds(pl.multiple_of(i * TILE, TILE), TILE)
            value = part(lambda d, s, rows: coming[d, s, rows, cols], arrived[block, :, cols])
            for d, s, rows in keep:
                blocks[0, d * 4 + s, rows, cols] = value[rows]
            return carry

        lax.fori_loop(0, HALF // TILE, tile, 0)
        value = part(lambda d, s, rows: coming_lane[d, s, rows, :], arrived_lane[block])
        for d, s, rows in keep:
            going_lane[d, s, rows, :] = value[rows]

    for n in range(NZ):
        sent(1, n)
    pltpu.make_async_copy(others, others, out_recv.at[1]).wait()
    load = pltpu.make_async_copy(tok_out, gd_rows, tok_sem)
    load.start()
    load.wait()

    def share_tiles(dx, store):
        def tile(i, carry):
            cols = pl.ds(pl.multiple_of(((x + dx) % NX) * SHARE + i * 256, 256), 256)
            store(i, contract(gd_rows[:, cols], both[...], 0, 0))
            return carry

        lax.fori_loop(0, SHARE // 256, tile, 0)

    gate_up_shares = []
    for dx in (2, 1, 3):

        def store_going(i, value):
            rows = pl.ds(pl.multiple_of((dx - 1) * SHARE + i * 256, 256), 256)
            w_gate_up[rows, :] = value.astype(jnp.bfloat16)

        share_tiles(dx, store_going)
        copy = remote(
            w_gate_up.at[pl.ds((dx - 1) * SHARE, SHARE), :], share_coming.at[dx - 1],
            share_send.at[dx - 1], share_recv.at[dx - 1], {"dp": (x + dx) % NX},
        )
        copy.start()
        gate_up_shares.append(copy)

    top, bottom, whole = slice(0, TOK), slice(TOK, PAIR), slice(0, PAIR)
    ready(0)
    partial(0, 0, (), ((0, 0, top), (1, 0, bottom)))
    chain_start(0, 0)
    chain_start(0, 1)
    for step in range(1, 4):
        for direction in (1, 0):
            n = 2 * step - 1 if direction == 1 else 2 * step
            ready(n)
            chain_recv(step - 1, direction)
            partial(n, step, (direction,), ((direction, step, whole),))
            chain_start(step, direction)

    def store_own(i, value):
        share_ref[pl.ds(pl.multiple_of(i * 256, 256), 256), :] = value

    share_tiles(0, store_own)
    for copy in gate_up_shares:
        copy.wait_recv()
    for n in range(NX - 1):
        share_ref[...] += share_coming[n].astype(jnp.float32)
    for direction in range(2):
        chain_sent(0, direction)
    ready(7)
    for direction in range(2):
        chain_recv(3, direction)
    partial(7, 4, (0, 1), ((0, 0, whole),))
    its = pl.ds(pl.multiple_of((1 - c) * TOK, TOK), TOK)
    swap = remote(going(0, 0).at[its, :], last, swap_send.at[0], swap_recv.at[0], partner)
    swap_lane = remote(going_lane.at[0, 0, its, :], last_lane, swap_send.at[1], swap_recv.at[1], partner)
    swap.start()
    swap_lane.start()
    out_ref[:, my_half] = blocks[0, 0, mine, :]
    swap_lane.wait_recv()
    dense = going_lane[0, 0, mine, :] + last_lane[...]
    first = lax.broadcasted_iota(jnp.int32, (TOK, TOK), 0)
    second = lax.broadcasted_iota(jnp.int32, (TOK, TOK), 1)
    dense = contract(dense, jnp.where(first == second, 1.0, 0.0).astype(jnp.bfloat16), 0, 0)
    row = lax.broadcasted_iota(jnp.int32, (128, TOK), 0)
    expert = ((row // 2) % NY) * (NZ * NC) + (row // 8) * NC + row % 2
    for k in range(TOPK):
        hit = ids_ref[k : k + 1, :] == expert
        picked = jnp.sum(jnp.where(hit, dense, 0.0), axis=0, keepdims=True)
        gate_ref[k : k + 1, :] = picked / gates_ref[k : k + 1, :]
    swap.wait_recv()
    out_ref[:, its_half] = last[...]
    for copy in shares + pairs + gate_up_shares + [swap, swap_lane]:
        copy.wait_send()
    for step in range(4):
        for direction in range(2):
            ring(1, step, direction).wait_send()
            ring(2, step, direction).wait_send()
            if step:
                chain_sent(step, direction)
    pltpu.make_async_copy(others, others, back_send).wait()
    lane = arrived_lane.at[pl.ds(0, NY - 1)]
    pltpu.make_async_copy(lane, lane, lane_send).wait()


ANY = pl.BlockSpec(memory_space=pl.ANY)
VMEM = pl.BlockSpec(memory_space=pltpu.VMEM)
DMA = pltpu.SemaphoreType.DMA


def bf16(*shape):
    return jax.ShapeDtypeStruct(shape, jnp.bfloat16)


def layer(ids, gates, d_output, tokens, saved, w_gate_up, w_down):
    scratch = [
        (NZ, NC, 128, TOK), (2, NZ, PAIR, HALF), (NZ, ROWS, HALF), (ROWS, PAIR), (NZ, ROWS, PAIR), (SLOTS, D),
        (SLOTS, 2 * FF), (D, 2 * FF), (FF, D), (SLOTS, FF), (SLOTS, 2 * FF), (SLOTS, D), (SLOTS, 128),
    ]
    more = [
        (NX - 1, FF, SHARE), (NX - 1, FF, SHARE), (NZ, ROWS, HALF), (NZ, ROWS, 128), (2, 4, PAIR, HALF),
        (2, 4, PAIR, 128), (2, 4, PAIR, 128), (TOK, HALF), (TOK, 128), (NX - 1, SHARE, 2 * FF),
    ]
    semaphores = [
        (2,), (3,), (3,), (3, 4, 2), (3, 4, 2), (2, 8), (2,), (2, 8), (3,), (NX - 1,), (NX - 1,),
        (), (8,), (), (8,), (2, 4), (2, 4), (2, 4), (2, 4), (2,), (2,), (), (NX - 1,), (NX - 1,),
    ]
    return pl.pallas_call(
        layer_kernel,
        out_shape=(
            bf16(SLOTS, D), bf16(TOK, D), jax.ShapeDtypeStruct((TOPK, TOK), jnp.float32),
            jax.ShapeDtypeStruct((SHARE, 2 * FF), jnp.float32), jax.ShapeDtypeStruct((FF, SHARE), jnp.float32),
        ),
        in_specs=[VMEM, VMEM, ANY, ANY, ANY, ANY, ANY],
        out_specs=(ANY, VMEM, VMEM, VMEM, VMEM),
        scratch_shapes=[pltpu.VMEM(shape, jnp.bfloat16) for shape in scratch]
        + [pltpu.VMEM((FF, SHARE), jnp.float32)]
        + [pltpu.VMEM(shape, jnp.bfloat16) for shape in more]
        + [DMA(shape) if shape else DMA for shape in semaphores],
        compiler_params=pltpu.CompilerParams(collective_id=0, has_side_effects=True, vmem_limit_bytes=67043328),
        name="layer",
    )(ids, gates, d_output, tokens, saved, w_gate_up, w_down)


def on_device(tokens, d_output, expert_ids, gate_weights, pre_acts, w_gate_up, w_down):
    ids, gates = expert_ids.T, gate_weights.T.astype(jnp.float32)
    _, token_grads, gate_grads, gate_up_share, down_share = layer(
        ids, gates, d_output, tokens, pre_acts[0, 0], w_gate_up[0], w_down[0]
    )
    return token_grads, gate_grads.T.astype(jnp.bfloat16), gate_up_share[None], down_share[None]


def solution(mesh):
    grid = Mesh(mesh.devices.reshape(NY, NZ, NC, NX), ("y", "z", "c", "dp"))
    expert = ("y", "z", "c")
    token = P(expert + ("dp",), None)
    return jax.shard_map(
        on_device,
        mesh=grid,
        in_specs=(
            token, token, token, token,
            P("dp", expert, None, None), P(expert, None, None), P(expert, None, None),
        ),
        out_specs=(token, token, P(expert, "dp", None), P(expert, None, "dp")),
        check_vma=False,
    )
```

time: 257 us -> 251 us (0.977)
  Pallas kernels: 248 us -> 242 us
    pallas_call x2 -> x1, Pallas kernels: 248 us -> 242 us  [layer(): pl.pallas_call(layer_kernel, out_shape=(bf16(SLOTS, D), bf16(TOK, D), jax...]
where the time goes in v3:
time: 251 us
  Pallas kernels  242 us (96%)
  local copies, waits for them, and re-layouts  5.41 us (2%)
  other arithmetic  2.6 us (1%)
    pallas_call x1, Pallas kernels, layer(): pl.pallas_call(layer_kernel, out_shape=(bf16(SLOTS, D), bf16(TOK, D), jax...  242 us
    unnamed x5, local copies, waits for them, and re-layouts  5.41 us

profile of v3, /device:TPU:1, one launch (start us, length us, event | category | flops | bytes accessed | tf_op | source)
XLA Modules:
  0.0 250.9 jit_solution(10658046654458697548)
XLA Ops:
  0.6 1.3 convert_bitcast_fusion.gates_ref
  1.9 242.2 %layer.1 = (bf16[1536,2048]{1,0:T(8,128)(2,1)}, bf16[128,2048]{1,0:T(8,128)(2,1)}, f32[8,128]{1,0:T(8,128)}, f32[512,768]{1,0:T(8,128)}, f32[384,512]{1,0:T(8,128)}) custom-call(s32[8,128]{1,0:T(8,128)} %bitcast.15, f32[8,128]{1,0:T(8,128)} %convert_bitcast_fusion.gates_ref, bf16[128,2048]{1,0:T(8,128)(2,1)} %d_ref.1, bf16[128,2048]{1,0:T(8,128)(2,1)} %t_ref.1, ...), custom_call_target="tpu_custom_call" | custom-call | tf_op jit(solution)/shard_map/layer/pallas_call | solution.py:438
  244.1 0.0 copy-start
  244.1 1.3 convert_bitcast_fusion.1
  245.5 1.9 copy.14
  247.3 2.7 %copy.15 = f32[1,512,768]{2,1,0:T(8,128)} copy(f32[1,512,768]{2,1,0:T(8,128)} %bitcast.13) | data formatting | bytes 3145728
  250.0 0.0 copy-done
  250.0 0.9 copy.16
Async XLA Ops:
  244.1 5.9 %copy-start = (f32[384,512]{1,0:T(8,128)S(1)}, f32[384,512]{1,0:T(8,128)}, u32[]{:S(2)}) copy-start(f32[384,512]{1,0:T(8,128)} %get-tuple-element.11) | copy-start | bytes 2359300

commit v4 on v3

--- a/solution.py
+++ b/solution.py
@@ -80,7 +80,7 @@
     down_own, down_going, down_coming, arrived, arrived_lane, coming, coming_lane, going_lane, last, last_lane, share_coming,
     load_sem, pair_send, pair_recv, ring_send, ring_recv, out_send, out_recv, own_sem, weight_sem, down_send, down_recv,
     back_send, back_recv, lane_send, lane_recv, sum_send, sum_recv, sum_lane_send, sum_lane_recv,
-    swap_send, swap_recv, tok_sem, share_send, share_recv,
+    swap_send, swap_recv, tok_sem, share_send, share_recv, final_send, final_recv,
 ):
     y, z, c = place()
     x = lax.axis_index("dp")
@@ -220,22 +220,31 @@
     lax.fori_loop(0, NY, expert_rows, 0)
     at = pl.ds(pl.multiple_of((y * NC + c) * SEG, SEG), SEG)
     order = (4, 5, 3, 6, 2, 7, 1, 0)
-    for n, dz in enumerate(order):
-        block = (z + dz) % NZ
+    pieces = [(n, 0, HALF) for n in range(6)] + [(6, 0, HALF // 2), (6, HALF // 2, HALF // 2), (7, 0, HALF)]
+
+    def send_piece(p):
+        n, begins, width = pieces[p]
+        block = (z + order[n]) % NZ
         for dy in (1, 3, 2, 0):
             for dc in range(NC):
                 py, pc = (y + dy) % NY, (c + dc) % NC
                 rows = pl.ds(pl.multiple_of(py * YROWS + block * SEG, SEG), SEG)
-                half = (route.at[rows, pl.ds(pl.multiple_of(pc * HALF, HALF), HALF)], arrived.at[block, at, :])
+                cols = pl.ds(pl.multiple_of(pc * HALF + begins, width), width)
+                half = (route.at[rows, cols], arrived.at[block, at, pl.ds(begins, width)])
+                if dy or dc:
+                    remote(*half, back_send, back_recv.at[p], {"y": py, "c": pc}).start()
+                else:
+                    pltpu.make_async_copy(*half, back_recv.at[p]).start()
+                if begins:
+                    continue
                 lane = (lanes.at[rows, :], arrived_lane.at[block, at, :])
-                if dy or dc:
-                    remote(*half, back_send, back_recv.at[n], {"y": py, "c": pc}).start()
-                else:
-                    pltpu.make_async_copy(*half, back_recv.at[n]).start()
                 if dy and dc == 0:
                     remote(*lane, lane_send, lane_recv.at[n], {"y": py, "c": pc}).start()
                 elif dc == 0:
                     pltpu.make_async_copy(*lane, lane_recv.at[n]).start()
+
+    for p in range(len(pieces)):
+        send_piece(p)
 
     def down_part(dx):
         cols = pl.ds(pl.multiple_of(((x + dx) % NX) * SHARE, SHARE), SHARE)
@@ -290,13 +299,15 @@
         for copy in chain(step, direction):
             copy.wait_send()
 
-    def ready(n):
+    def ready(p):
+        n, begins, width = pieces[p]
         block = (z + order[n]) % NZ
-        half, lane = arrived.at[block], arrived_lane.at[block, : ROWS // 2]
-        pltpu.make_async_copy(half, half, back_recv.at[n]).wait()
-        pltpu.make_async_copy(lane, lane, lane_recv.at[n]).wait()
-
-    def partial(n, step, directions, keep):
+        half, lane = arrived.at[block, :, pl.ds(begins, width)], arrived_lane.at[block, : ROWS // 2]
+        pltpu.make_async_copy(half, half, back_recv.at[p]).wait()
+        if not begins:
+            pltpu.make_async_copy(lane, lane, lane_recv.at[n]).wait()
+
+    def partial(n, step, directions, keep, first_tile=0, tiles=HALF // TILE):
         block = (z + order[n]) % NZ
 
         def part(came, rows):
@@ -319,7 +330,9 @@
                 blocks[0, d * 4 + s, rows, cols] = value[rows]
             return carry
 
-        lax.fori_loop(0, HALF // TILE, tile, 0)
+        lax.fori_loop(first_tile, first_tile + tiles, tile, 0)
+        if first_tile:
+            return
         value = part(lambda d, s, rows: coming_lane[d, s, rows, :], arrived_lane[block])
         for d, s, rows in keep:
             going_lane[d, s, rows, :] = value[rows]
@@ -353,6 +366,30 @@
         )
         copy.start()
         gate_up_shares.append(copy)
+
+    final = [
+        remote(
+            going(0, 3).at[:, pl.ds(i * (HALF // 2), HALF // 2)], coming.at[0, 3, :, pl.ds(i * (HALF // 2), HALF // 2)],
+            final_send.at[i], final_recv.at[i], up,
+        )
+        for i in range(2)
+    ]
+    final.append(
+        remote(
+            going_lane.at[0, 3], coming_lane.at[0, 3], sum_lane_send.at[0, 3], sum_lane_recv.at[0, 3], up
+        )
+    )
+
+    def store_own(i, value):
+        share_ref[pl.ds(pl.multiple_of(i * 256, 256), 256), :] = value
+
+    share_tiles(0, store_own)
+
+    def gather_shares():
+        for copy in gate_up_shares:
+            copy.wait_recv()
+        for n in range(NX - 1):
+            share_ref[...] += share_coming[n].astype(jnp.float32)
 
     top, bottom, whole = slice(0, TOK), slice(TOK, PAIR), slice(0, PAIR)
     ready(0)
@@ -362,24 +399,26 @@
     for step in range(1, 4):
         for direction in (1, 0):
             n = 2 * step - 1 if direction == 1 else 2 * step
+            if n == 5:
+                gather_shares()
             ready(n)
             chain_recv(step - 1, direction)
-            partial(n, step, (direction,), ((direction, step, whole),))
-            chain_start(step, direction)
-
-    def store_own(i, value):
-        share_ref[pl.ds(pl.multiple_of(i * 256, 256), 256), :] = value
-
-    share_tiles(0, store_own)
-    for copy in gate_up_shares:
-        copy.wait_recv()
-    for n in range(NX - 1):
-        share_ref[...] += share_coming[n].astype(jnp.float32)
+            if n < 6:
+                partial(n, step, (direction,), ((direction, step, whole),))
+                chain_start(step, direction)
+                continue
+            partial(n, step, (direction,), ((direction, step, whole),), 0, HALF // TILE // 2)
+            final[0].start()
+            final[2].start()
+            ready(7)
+            partial(n, step, (direction,), ((direction, step, whole),), HALF // TILE // 2, HALF // TILE // 2)
+            final[1].start()
     for direction in range(2):
         chain_sent(0, direction)
-    ready(7)
-    for direction in range(2):
-        chain_recv(3, direction)
+    ready(8)
+    chain_recv(3, 1)
+    for copy in final:
+        copy.wait_recv()
     partial(7, 4, (0, 1), ((0, 0, whole),))
     its = pl.ds(pl.multiple_of((1 - c) * TOK, TOK), TOK)
     swap = remote(going(0, 0).at[its, :], last, swap_send.at[0], swap_recv.at[0], partner)
@@ -406,8 +445,10 @@
         for direction in range(2):
             ring(1, step, direction).wait_send()
             ring(2, step, direction).wait_send()
-            if step:
+            if step and (step, direction) != (3, 0):
                 chain_sent(step, direction)
+    for copy in final:
+        copy.wait_send()
     pltpu.make_async_copy(others, others, back_send).wait()
     lane = arrived_lane.at[pl.ds(0, NY - 1)]
     pltpu.make_async_copy(lane, lane, lane_send).wait()
@@ -433,7 +474,7 @@
     ]
     semaphores = [
         (2,), (3,), (3,), (3, 4, 2), (3, 4, 2), (2, 8), (2,), (2, 8), (3,), (NX - 1,), (NX - 1,),
-        (), (8,), (), (8,), (2, 4), (2, 4), (2, 4), (2, 4), (2,), (2,), (), (NX - 1,), (NX - 1,),
+        (), (9,), (), (8,), (2, 4), (2, 4), (2, 4), (2, 4), (2,), (2,), (), (NX - 1,), (NX - 1,), (2,), (2,),
     ]
     return pl.pallas_call(
         layer_kernel,
@@ -452,12 +493,31 @@
     )(ids, gates, d_output, tokens, saved, w_gate_up, w_down)
 
 
+def finish_kernel(rows_ref, gate_ref, share_ref, down_ref, rows_out, gate_out, share_out, down_out):
+    rows_out[...] = rows_ref[...]
+    gate_out[...] = gate_ref[...].astype(jnp.bfloat16)
+    share_out[...] = share_ref[...]
+    down_out[...] = down_ref[...]
+
+
+def finish(*results):
+    rows, gate, share, down = (jax.ShapeDtypeStruct(r.shape, r.dtype) for r in results)
+    return pl.pallas_call(
+        finish_kernel,
+        out_shape=(rows, bf16(TOPK, TOK), share, down),
+        in_specs=[VMEM] * 4,
+        out_specs=(VMEM,) * 4,
+        name="finish",
+    )(*results)
+
+
 def on_device(tokens, d_output, expert_ids, gate_weights, pre_acts, w_gate_up, w_down):
     ids, gates = expert_ids.T, gate_weights.T.astype(jnp.float32)
     _, token_grads, gate_grads, gate_up_share, down_share = layer(
         ids, gates, d_output, tokens, pre_acts[0, 0], w_gate_up[0], w_down[0]
     )
-    return token_grads, gate_grads.T.astype(jnp.bfloat16), gate_up_share[None], down_share[None]
+    token_grads, gate_grads, gate_up_share, down_share = finish(token_grads, gate_grads, gate_up_share, down_share)
+    return token_grads, gate_grads.T, gate_up_share[None], down_share[None]
 
 
 def solution(mesh):

time: 251 us -> 246 us (0.980)
  local copies, waits for them, and re-layouts: 5.41 us -> 0 us
    unnamed x5 -> x0, local copies, waits for them, and re-layouts: 5.41 us -> none
    pallas_call x0 -> x1, Pallas kernels: none -> 3.38 us  [finish(): pl.pallas_call(finish_kernel, out_shape=(rows, bf16(TOPK, TOK), share, do...]
where the time goes in v4:
time: 246 us; the launch traced here: 245 us
  Pallas kernels  243 us (99%)
    pallas_call x1, Pallas kernels, layer(): pl.pallas_call(layer_kernel, out_shape=(bf16(SLOTS, D), bf16(TOK, D), jax...  240 us

profile of v4, /device:TPU:1, one launch (start us, length us, event | category | flops | bytes accessed | tf_op | source)
XLA Modules:
  0.0 245.4 jit_solution(689565358474701824)
XLA Ops:
  0.6 1.3 convert_bitcast_fusion.gates_ref
  1.9 240.1 %layer.1 = (bf16[1536,2048]{1,0:T(8,128)(2,1)}, bf16[128,2048]{1,0:T(8,128)(2,1)}, f32[8,128]{1,0:T(8,128)}, f32[512,768]{1,0:T(8,128)}, f32[384,512]{1,0:T(8,128)}) custom-call(s32[8,128]{1,0:T(8,128)} %bitcast.12, f32[8,128]{1,0:T(8,128)} %convert_bitcast_fusion.gates_ref, bf16[128,2048]{1,0:T(8,128)(2,1)} %d_ref.1, bf16[128,2048]{1,0:T(8,128)(2,1)} %t_ref.1, ...), custom_call_target="tpu_custom_call" | custom-call | tf_op jit(solution)/shard_map/layer/pallas_call | solution.py:479
  242.0 3.4 %finish.1 = (bf16[128,2048]{1,0:T(8,128)(2,1)}, bf16[8,128]{1,0:T(8,128)(2,1)}, f32[512,768]{1,0:T(8,128)}, f32[384,512]{1,0:T(8,128)}) custom-call(bf16[128,2048]{1,0:T(8,128)(2,1)} %get-tuple-element.12.rows_ref, f32[8,128]{1,0:T(8,128)} %get-tuple-element.13.gate_ref, f32[512,768]{1,0:T(8,128)} %get-tuple-element.14.share_ref, ...), custom_call_target="tpu_custom_call" | custom-call | tf_op jit(solution)/shard_map/finish/pallas_call | solution.py:505

commit v5 on v4

--- a/solution.py
+++ b/solution.py
@@ -28,7 +28,7 @@
     )
 
 
-def plane_barrier(y, z, c):
+def greet(y, z, c):
     barrier = pltpu.get_barrier_semaphore()
     for dy in range(NY):
         for dc in range(NC):
@@ -44,7 +44,6 @@
     x = lax.axis_index("dp")
     for dx in range(1, NX):
         pl.semaphore_signal(barrier, inc=1, device_id={"dp": (x + dx) % NX}, device_id_type=MESH)
-    pl.semaphore_wait(barrier, PEERS - 1 + 2 + NX - 1)
 
 
 def remote(src, dst, send_sem, recv_sem, where):
@@ -97,6 +96,7 @@
     ]
     for load in loads:
         load.start()
+    greet(y, z, c)
     weights = [
         pltpu.make_async_copy(src, dst, weight_sem.at[n])
         for n, (src, dst) in enumerate(((saved_hbm, saved), (down_hbm, w_down), (gate_up_hbm, w_gate_up)))
@@ -105,7 +105,7 @@
         copy.start()
     arrived_lane[...] = jnp.zeros_like(arrived_lane)
     meta[z, c] = table(ids_ref[...], gates_ref[...], c)
-    plane_barrier(y, z, c)
+    pl.semaphore_wait(pltpu.get_barrier_semaphore(), PEERS - 1 + 2 + NX - 1)
     pairs = [
         remote(meta.at[z, c], meta.at[z, c], pair_send.at[2], pair_recv.at[2], partner),
         remote(sources[0].at[:, its_half], blocks.at[0, z, mine, :], pair_send.at[0], pair_recv.at[0], partner),
@@ -220,7 +220,7 @@
     lax.fori_loop(0, NY, expert_rows, 0)
     at = pl.ds(pl.multiple_of((y * NC + c) * SEG, SEG), SEG)
     order = (4, 5, 3, 6, 2, 7, 1, 0)
-    pieces = [(n, 0, HALF) for n in range(6)] + [(6, 0, HALF // 2), (6, HALF // 2, HALF // 2), (7, 0, HALF)]
+    pieces = [(n, 0, HALF) for n in range(6)] + [(n, i * (HALF // 2), HALF // 2) for n in (6, 7) for i in range(2)]
 
     def send_piece(p):
         n, begins, width = pieces[p]
@@ -415,16 +415,21 @@
             final[1].start()
     for direction in range(2):
         chain_sent(0, direction)
-    ready(8)
+    its = pl.ds(pl.multiple_of((1 - c) * TOK, TOK), TOK)
+    swap_lane = remote(going_lane.at[0, 0, its, :], last_lane, swap_send.at[2], swap_recv.at[2], partner)
     chain_recv(3, 1)
-    for copy in final:
-        copy.wait_recv()
-    partial(7, 4, (0, 1), ((0, 0, whole),))
-    its = pl.ds(pl.multiple_of((1 - c) * TOK, TOK), TOK)
-    swap = remote(going(0, 0).at[its, :], last, swap_send.at[0], swap_recv.at[0], partner)
-    swap_lane = remote(going_lane.at[0, 0, its, :], last_lane, swap_send.at[1], swap_recv.at[1], partner)
-    swap.start()
-    swap_lane.start()
+    final[2].wait_recv()
+    swaps = []
+    for i in range(2):
+        final[i].wait_recv()
+        ready(8 + i)
+        partial(7, 4, (0, 1), ((0, 0, whole),), i * (HALF // TILE // 2), HALF // TILE // 2)
+        cols = pl.ds(i * (HALF // 2), HALF // 2)
+        swap = remote(going(0, 0).at[its, cols], last.at[:, cols], swap_send.at[i], swap_recv.at[i], partner)
+        swap.start()
+        swaps.append(swap)
+        if i == 0:
+            swap_lane.start()
     out_ref[:, my_half] = blocks[0, 0, mine, :]
     swap_lane.wait_recv()
     dense = going_lane[0, 0, mine, :] + last_lane[...]
@@ -437,9 +442,10 @@
         hit = ids_ref[k : k + 1, :] == expert
         picked = jnp.sum(jnp.where(hit, dense, 0.0), axis=0, keepdims=True)
         gate_ref[k : k + 1, :] = picked / gates_ref[k : k + 1, :]
-    swap.wait_recv()
+    for swap in swaps:
+        swap.wait_recv()
     out_ref[:, its_half] = last[...]
-    for copy in shares + pairs + gate_up_shares + [swap, swap_lane]:
+    for copy in shares + pairs + gate_up_shares + swaps + [swap_lane]:
         copy.wait_send()
     for step in range(4):
         for direction in range(2):
@@ -474,7 +480,7 @@
     ]
     semaphores = [
         (2,), (3,), (3,), (3, 4, 2), (3, 4, 2), (2, 8), (2,), (2, 8), (3,), (NX - 1,), (NX - 1,),
-        (), (9,), (), (8,), (2, 4), (2, 4), (2, 4), (2, 4), (2,), (2,), (), (NX - 1,), (NX - 1,), (2,), (2,),
+        (), (10,), (), (8,), (2, 4), (2, 4), (2, 4), (2, 4), (3,), (3,), (), (NX - 1,), (NX - 1,), (2,), (2,),
     ]
     return pl.pallas_call(
         layer_kernel,

time: 246 us -> 244 us (level)
  no operation moved by 1% of the time
where the time goes in v5:
time: 244 us
  Pallas kernels  242 us (99%)
    pallas_call x1, Pallas kernels, layer(): pl.pallas_call(layer_kernel, out_shape=(bf16(SLOTS, D), bf16(TOK, D), jax...  239 us

profile of v5, /device:TPU:1, one launch (start us, length us, event | category | flops | bytes accessed | tf_op | source)
XLA Modules:
  0.0 243.8 jit_solution(2923584581360412254)
XLA Ops:
  0.6 1.3 convert_bitcast_fusion.gates_ref
  1.9 238.5 %layer.1 = (bf16[1536,2048]{1,0:T(8,128)(2,1)}, bf16[128,2048]{1,0:T(8,128)(2,1)}, f32[8,128]{1,0:T(8,128)}, f32[512,768]{1,0:T(8,128)}, f32[384,512]{1,0:T(8,128)}) custom-call(s32[8,128]{1,0:T(8,128)} %bitcast.12, f32[8,128]{1,0:T(8,128)} %convert_bitcast_fusion.gates_ref, bf16[128,2048]{1,0:T(8,128)(2,1)} %d_ref.1, bf16[128,2048]{1,0:T(8,128)(2,1)} %t_ref.1, ...), custom_call_target="tpu_custom_call" | custom-call | tf_op jit(solution)/shard_map/layer/pallas_call | solution.py:485
  240.4 3.4 %finish.1 = (bf16[128,2048]{1,0:T(8,128)(2,1)}, bf16[8,128]{1,0:T(8,128)(2,1)}, f32[512,768]{1,0:T(8,128)}, f32[384,512]{1,0:T(8,128)}) custom-call(bf16[128,2048]{1,0:T(8,128)(2,1)} %get-tuple-element.12.rows_ref, f32[8,128]{1,0:T(8,128)} %get-tuple-element.13.gate_ref, f32[512,768]{1,0:T(8,128)} %get-tuple-element.14.share_ref, ...), custom_call_target="tpu_custom_call" | custom-call | tf_op jit(solution)/shard_map/finish/pallas_call | solution.py:511
